TPU v7x, 512 devices: a whole 4x8x8 slice. The times are simulated.
512 devices in a mesh: fluid: 64 (over z, y), sub: 4 (over x), struct: 2 (over core).
Axes of the slice: x: 4, y: 8, z: 8, core: 2. Of those that a mesh axis runs over, the one named last changes fastest.
Arguments:
- velocity: float32 [256, 64, 3, 256], P('fluid', 'sub'), may hold values from -6 to 6
- pressure: float32 [256, 64, 256], P('fluid', 'sub'), may hold values from -6 to 6
- viscosity: float32 [256, 64, 256], P('fluid', 'sub'), may hold values from 0.02 to 0.15
- marker_force: float32 [32768, 3, 128], P(('fluid', 'sub', 'struct')), may hold values from -24 to 24
- marker_offset: float32 [32768, 3, 128], P(('fluid', 'sub', 'struct')), may hold values from 0 to 1
- cell_base: int32 [32768, 3, 128], P(('fluid', 'sub', 'struct')), may hold values from 0 to 253, as said below
- block_slab: int32 [32768, 1], P(('fluid', 'sub', 'struct')), may hold values from 0 to 63; in each aligned block of 64 rows (0 to 63, 64 to 127, ...) at most 2 rows name the same one
Outputs:
- new_velocity: float32 [256, 64, 3, 256], P('fluid', 'sub')
- marker_velocity: float32 [32768, 3, 128], P(('fluid', 'sub', 'struct'))
Inputs may be any that keep to these rules, and one draw needn't show every extreme that they name: cell_base[b,0,m] lies in 0 to 3, cell_base[b,1,m] in 0 to 15 and cell_base[b,2,m] in 1 to 253. `block_slab`: within the 64 blocks of one device no slab is named more than 2 times.
All inputs are finite; a program needn't handle non-finite values.
Results may differ from a plain program's by a relative error of at most 0.0034.
Values may be sent and summed in bfloat16 or wider, within the bound.
No kernel may reach another device: no remote copies, remote signals or barrier semaphores. Data moves between devices by JAX's collectives and lax.ppermute only.
A program may use at most 64 MiB of HBM per device.

v0:
```python
import math

import jax
import jax.numpy as jnp
from jax import lax
from jax.sharding import PartitionSpec as P

neighbour_steps = ((1, 0, 0), (-1, 0, 0), (0, 1, 0), (0, -1, 0), (0, 0, 1), (0, 0, -1))


def with_halo(cells, sides, width):
    for axis, dim in sides:
        count = lax.axis_size(axis)
        ends = count - 1
        head = lax.slice_in_dim(cells, 0, width, axis=dim)
        tail = lax.slice_in_dim(cells, cells.shape[dim] - width, cells.shape[dim], axis=dim)
        cells = jnp.concatenate(
            [
                lax.ppermute(tail, axis, [(i, (i + 1) % count) for i in range(ends)]),
                cells,
                lax.ppermute(head, axis, [((i + 1) % count, i) for i in range(ends)]),
            ],
            axis=dim,
        )
    return cells


def kernel_weight(distance):
    inside = jnp.minimum(distance, 1.0)
    beyond = jnp.clip(distance - 1.0, 0.0, 1.0)
    inner = (3.0 - 2.0 * inside + jnp.sqrt(1.0 + 4.0 * inside - 4.0 * inside * inside)) * 0.125
    outer = (3.0 - 2.0 * beyond - jnp.sqrt(1.0 + 4.0 * beyond - 4.0 * beyond * beyond)) * 0.125
    return jnp.where(distance < 1.0, inner, outer)


def offset(array, first, second, third):
    extent_first = array.shape[0] - 2
    extent_second = array.shape[1] - 2
    extent_third = array.shape[-1] - 2
    return array[
        1 + first : 1 + first + extent_first,
        1 + second : 1 + second + extent_second,
        ...,
        1 + third : 1 + third + extent_third,
    ]


def momentum(old_pad, force):
    velocity_pad = old_pad[:, :, 0:3]
    pressure_pad = old_pad[:, :, 3]
    viscosity_pad = old_pad[:, :, 4]
    centre = offset(velocity_pad, 0, 0, 0)
    viscosity_centre = offset(viscosity_pad, 0, 0, 0)[:, :, None]
    pressure_centre = offset(pressure_pad, 0, 0, 0)
    viscous = jnp.zeros_like(centre)
    for neighbour in neighbour_steps:
        neighbour_value = offset(velocity_pad, neighbour[0], neighbour[1], neighbour[2])
        face_viscosity = 0.5 * (
            viscosity_centre
            + offset(viscosity_pad, neighbour[0], neighbour[1], neighbour[2])[:, :, None]
        )
        viscous = viscous + face_viscosity * (neighbour_value - centre)
    gradient = jnp.stack(
        [
            offset(pressure_pad, 1, 0, 0) - pressure_centre,
            offset(pressure_pad, 0, 1, 0) - pressure_centre,
            offset(pressure_pad, 0, 0, 1) - pressure_centre,
        ],
        axis=2,
    )
    return centre + 0.5 * (viscous - gradient + force)


def fold_axis(rimmed, axis):
    length = rimmed.shape[axis] - 7
    core = lax.slice_in_dim(rimmed, 3, 3 + length, axis=axis)
    lower = lax.slice_in_dim(rimmed, 0, 2, axis=axis)
    upper = lax.slice_in_dim(rimmed, length + 5, length + 6, axis=axis)
    lower_shape = list(core.shape)
    lower_shape[axis] = length - 2
    upper_shape = list(core.shape)
    upper_shape[axis] = length - 1
    lower_full = jnp.concatenate([lower, jnp.zeros(lower_shape, core.dtype)], axis=axis)
    upper_full = jnp.concatenate([jnp.zeros(upper_shape, core.dtype), upper], axis=axis)
    return core + lower_full + upper_full


def fold_rims(padded):
    rimmed = with_halo(padded, (("fluid", 0), ("sub", 1)), 2)
    return fold_axis(fold_axis(rimmed, 0), 1)


def body(velocity, pressure, viscosity, marker_force, marker_offset, cell_base, block_slab):
    extent_x = velocity.shape[0]
    extent_y = velocity.shape[1]
    depth = velocity.shape[3]
    blocks = marker_force.shape[0]
    markers = marker_force.shape[2]
    slabs = lax.axis_size("fluid")
    capacity = 2 * blocks // slabs
    slots = slabs * capacity
    group = math.gcd(slots, max(1, 1024 // markers))
    turns = slots // group
    stacked = jnp.concatenate([velocity, pressure[:, :, None], viscosity[:, :, None]], axis=2)
    old_rim = with_halo(stacked, (("fluid", 0), ("sub", 1)), 1)
    old_pad = jnp.pad(old_rim, ((0, 0), (0, 0), (0, 0), (1, 1)))
    target = block_slab[:, 0]
    chosen = (target[:, None] == jnp.arange(slabs, dtype=jnp.int32)[None, :]).astype(jnp.int32)
    earlier = jnp.cumsum(chosen, axis=0) - chosen
    place_in = jnp.sum(earlier * chosen, axis=1)
    position = target * capacity + place_in
    coords = cell_base.astype(jnp.float32) + marker_offset
    payload = jnp.concatenate([coords, marker_force], axis=1)
    outgoing = jnp.zeros((slots, 6, markers), jnp.float32).at[position].set(payload)
    arriving = lax.all_to_all(
        outgoing.reshape(slabs, capacity, 6, markers),
        "fluid",
        split_axis=0,
        concat_axis=0,
        tiled=True,
    )
    grouped = arriving.reshape(turns, group, 6, markers)
    first_cells = jnp.arange(extent_x + 3, dtype=jnp.float32) - 1.0
    second_cells = jnp.arange(extent_y + 3, dtype=jnp.float32) - 1.0
    depth_cells = jnp.arange(depth, dtype=jnp.float32)

    def weights(places):
        along_first = kernel_weight(jnp.abs(first_cells[None, :, None] - places[:, 0:1, :]))
        along_second = kernel_weight(jnp.abs(second_cells[None, :, None] - places[:, 1:2, :]))
        along_depth = kernel_weight(jnp.abs(depth_cells[None, None, :] - places[:, 2, :, None]))
        return (along_first, along_second, along_depth)

    def spread_turn(total, piece):
        along_first, along_second, along_depth = weights(piece[:, 0:3])
        plane = (
            (along_first[:, :, None, :] * along_second[:, None, :, :])
            .astype(jnp.bfloat16)
            .reshape(group, -1, markers)
        )
        pushes = jnp.transpose(piece[:, 3:6, :], (0, 2, 1))
        loaded = (
            (pushes[:, :, :, None] * along_depth[:, :, None, :])
            .astype(jnp.bfloat16)
            .reshape(group, markers, 3 * depth)
        )
        term = lax.dot_general(
            plane, loaded, (((0, 2), (0, 1)), ((), ())), preferred_element_type=jnp.float32
        )
        return (total + term, None)

    spread_flat, _ = lax.scan(
        spread_turn, jnp.zeros(((extent_x + 3) * (extent_y + 3), 3 * depth), jnp.float32), grouped
    )
    spread_pad = spread_flat.reshape(extent_x + 3, extent_y + 3, 3, depth)
    total_force = lax.psum(spread_pad, "struct")
    total_force = fold_rims(total_force)
    fresh = momentum(old_pad, total_force)
    rounded = fresh.astype(jnp.bfloat16)
    rim_velocity = with_halo(rounded, (("fluid", 0), ("sub", 1)), 2)
    flat_field = rim_velocity[1:, 1:].reshape(-1, depth)

    def sample_turn(piece):
        along_first, along_second, along_depth = weights(piece[:, 0:3])
        depth_weight = along_depth.astype(jnp.bfloat16)
        partial_sum = lax.dot_general(
            flat_field, depth_weight, (((1,), (2,)), ((), ())), preferred_element_type=jnp.float32
        )
        partial_sum = partial_sum.reshape(extent_x + 3, extent_y + 3, 3, group, markers)
        plane = along_first[:, :, None, :] * along_second[:, None, :, :]
        return jnp.einsum("gxym,xycgm->gcm", plane, partial_sum, precision=lax.Precision.HIGHEST)

    sampled = lax.map(sample_turn, grouped).reshape(slabs, capacity, 3, markers)
    returned = lax.all_to_all(sampled, "fluid", split_axis=0, concat_axis=0, tiled=True).reshape(
        slots, 3, markers
    )
    marker_velocity = returned[position]
    return (fresh, marker_velocity)


def solution(mesh):
    return jax.shard_map(
        body,
        mesh=mesh,
        in_specs=(
            P("fluid", "sub", None, None),
            P("fluid", "sub", None),
            P("fluid", "sub", None),
            P(("fluid", "sub", "struct"), None, None),
            P(("fluid", "sub", "struct"), None, None),
            P(("fluid", "sub", "struct"), None, None),
            P(("fluid", "sub", "struct"), None),
        ),
        out_specs=(P("fluid", "sub", None, None), P(("fluid", "sub", "struct"), None, None)),
        check_vma=False,
    )
```

profile of v0, /device:TPU:6, one launch (start us, length us, event | category | flops | bytes accessed | tf_op | source)
XLA Modules:
  0.0 259.4 jit_solution(9664407997614824740)
XLA Ops:
  11.6 2.4 scatter_fusion
  15.0 16.6 %all-to-all-start = ((f32[64,2,6,128]{3,1,2,0:T(2,128)}), f32[64,2,6,128]{3,1,2,0:T(2,128)S(1)}, u32[]{:S(2)}, u32[]{:S(2)}) async-start(f32[64,2,6,128]{3,1,2,0:T(2,128)} %copy.97), calls=%async_computation | async-start | bytes 786432 | tf_op jit(solution)/shard_map/all_to_all | solution.py:115
  33.0 4.6 %collective-permute-start = (f32[1,16,5,256]{3,1,0,2:T(8,128)S(1)}, f32[1,16,5,256]{3,1,0,2:T(8,128)S(1)}, u32[]{:S(2)}, u32[]{:S(2)}) collective-permute-start(f32[1,16,5,256]{3,1,0,2:T(8,128)S(1)} %get-tuple-element.303), channel_id=1, source_target_pairs={{0,8},{8,16},{16,24},{24,32},{32,40},{40,48},{48,56},{56,64},{64,7... | collective-permute-start | bytes 245768 | tf_op jit(solution)/shard_map/ppermute | solution.py:19
  37.5 5.7 %collective-permute-done.1 = f32[1,16,5,256]{3,1,0,2:T(8,128)S(1)} collective-permute-done((f32[1,16,5,256]{3,1,0,2:T(8,128)S(1)}, f32[1,16,5,256]{3,1,0,2:T(8,128)S(1)}, u32[]{:S(2)}, u32[]{:S(2)}) %collective-permute-start.1) | collective-permute-done | bytes 81952 | tf_op jit(solution)/shard_map/ppermute | solution.py:21
  43.3 2.7 %collective-permute-start.3 = (f32[6,1,5,256]{3,1,0,2:T(1,128)S(1)}, f32[6,1,5,256]{3,1,0,2:T(1,128)S(1)}, u32[]{:S(2)}, u32[]{:S(2)}) collective-permute-start(f32[6,1,5,256]{3,1,0,2:T(1,128)S(1)} %get-tuple-element.302), channel_id=1, source_target_pairs={{2,0},{4,2},{6,4},{3,1},{5,3},{7,5},{10,8},{12,10},{14,12},{11,9},... | collective-permute-start | bytes 92168 | tf_op jit(solution)/shard_map/ppermute | solution.py:21
  47.4 2.1 all-to-all-done
  49.6 45.7 %while.29 = (s32[]{:T(128)}, f32[133,768]{1,0:T(8,128)S(1)}, f32[16,8,6,128]{3,1,2,0:T(8,128)S(1)}, s32[]{:T(128)}, s32[]{:T(128)}) while((s32[]{:T(128)}, f32[133,768]{1,0:T(8,128)S(1)}, f32[16,8,6,128]{3,1,2,0:T(8,128)S(1)}, s32[]{:T(128)}, s32[]{:T(128)}) %tuple.104), condition=%wide.region_4.5_spmd.clone, body=%wide.region_3.4_spmd.clone.sunk | while | flops 217882144 | bytes 6965539 | solution.py:151
  97.0 34.0 %all-reduce.5.cloned.1.call-done = f32[7,19,3,256]{3,2,1,0:T(4,128)} async-done(((f32[7,19,3,256]{3,2,1,0:T(4,128)}), f32[7,19,3,256]{3,2,1,0:T(4,128)}) %all-reduce.5.cloned.1.call-update) | async-done | bytes 408592 | tf_op jit(solution)/shard_map/psum | solution.py:155
  132.2 3.4 %collective-permute-start.4 = (f32[2,19,3,256]{3,2,1,0:T(4,128)S(1)}, f32[2,19,3,256]{3,2,1,0:T(4,128)S(1)}, u32[]{:S(2)}, u32[]{:S(2)}) collective-permute-start(f32[2,19,3,256]{3,2,1,0:T(4,128)S(1)} %get-tuple-element.300), channel_id=1, source_target_pairs={{0,8},{8,16},{16,24},{24,32},{32,40},{40,48},{48,56},{56,64},{64,7... | collective-permute-start | bytes 350216 | tf_op jit(solution)/shard_map/ppermute | solution.py:19
  137.1 2.1 collective-permute-done.4
  139.4 4.2 %collective-permute-done.5 = f32[2,19,3,256]{3,2,1,0:T(4,128)S(1)} collective-permute-done((f32[2,19,3,256]{3,2,1,0:T(4,128)S(1)}, f32[2,19,3,256]{3,2,1,0:T(4,128)S(1)}, u32[]{:S(2)}, u32[]{:S(2)}) %collective-permute-start.5) | collective-permute-done | bytes 116768 | tf_op jit(solution)/shard_map/ppermute | solution.py:21
  143.7 2.8 %collective-permute-start.7 = (f32[11,2,3,256]{3,2,1,0:T(4,128)S(1)}, f32[11,2,3,256]{3,2,1,0:T(4,128)S(1)}, u32[]{:S(2)}, u32[]{:S(2)}) collective-permute-start(f32[11,2,3,256]{3,2,1,0:T(4,128)S(1)} %get-tuple-element.298), channel_id=1, source_target_pairs={{2,0},{4,2},{6,4},{3,1},{5,3},{7,5},{10,8},{12,10},{14,12},{11,9},... | collective-permute-start | bytes 202760 | tf_op jit(solution)/shard_map/ppermute | solution.py:21
  148.6 4.3 %collective-permute-done.6 = f32[11,2,3,256]{3,2,1,0:T(4,128)S(1)} collective-permute-done((f32[11,2,3,256]{3,2,1,0:T(4,128)S(1)}, f32[11,2,3,256]{3,2,1,0:T(4,128)S(1)}, u32[]{:S(2)}, u32[]{:S(2)}) %collective-permute-start.6) | collective-permute-done | bytes 67616 | tf_op jit(solution)/shard_map/ppermute | solution.py:19
  155.6 4.5 %collective-permute-start.8 = (bf16[2,16,3,256]{3,2,1,0:T(4,128)(2,1)S(1)}, bf16[2,16,3,256]{3,2,1,0:T(4,128)(2,1)S(1)}, u32[]{:S(2)}, u32[]{:S(2)}) collective-permute-start(bf16[2,16,3,256]{3,2,1,0:T(4,128)(2,1)S(1)} %get-tuple-element.316), channel_id=1, source_target_pairs={{0,8},{8,16},{16,24},{24,32},{32,40},{40,48},{48,56},{56,64},{64,7... | collective-permute-start | bytes 147464 | tf_op jit(solution)/shard_map/ppermute | solution.py:19
  162.1 2.5 collective-permute-start.11
  166.2 4.2 %collective-permute-done.10 = bf16[8,2,3,256]{3,2,1,0:T(4,128)(2,1)S(1)} collective-permute-done((bf16[8,2,3,256]{3,2,1,0:T(4,128)(2,1)S(1)}, bf16[8,2,3,256]{3,2,1,0:T(4,128)(2,1)S(1)}, u32[]{:S(2)}, u32[]{:S(2)}) %collective-permute-start.10) | collective-permute-done | bytes 24608 | tf_op jit(solution)/shard_map/ppermute | solution.py:19
  170.8 47.2 %while.28 = (s32[]{:T(128)}, f32[16,8,3,128]{3,2,1,0:T(4,128)S(1)}, f32[16,8,6,128]{3,1,2,0:T(8,128)S(1)}, bf16[399,256]{1,0:T(8,128)(2,1)S(1)}, s32[]{:T(128)}) while((s32[]{:T(128)}, f32[16,8,3,128]{3,2,1,0:T(4,128)S(1)}, f32[16,8,6,128]{3,1,2,0:T(8,128)S(1)}, bf16[399,256]{1,0:T(8,128)(2,1)S(1)}, s32[]{:T(128)}) %tuple.112), condition=%wide.region_7.8_spmd.clone, body=%wide.region_6.7_spmd.clone.sunk | while | flops 217045008 | bytes 9260829 | solution.py:172
  173.8 1.6 convolution_bitcast_fusion.3
  182.7 1.6 convolution_bitcast_fusion.3
  191.5 1.6 convolution_bitcast_fusion.3
  200.4 1.6 convolution_bitcast_fusion.3
  209.2 1.6 convolution_bitcast_fusion.3
  218.8 19.2 %all-to-all-start.1 = ((f32[64,2,3,128]{3,1,2,0:T(2,128)}), f32[64,2,3,128]{3,1,2,0:T(2,128)S(1)}, u32[]{:S(2)}, u32[]{:S(2)}) async-start(f32[64,2,3,128]{3,1,2,0:T(2,128)} %copy.103), calls=%async_computation.1 | async-start | bytes 393216 | tf_op jit(solution)/shard_map/all_to_all | solution.py:173
  238.8 12.4 %all-to-all-done.1 = f32[64,2,3,128]{3,1,2,0:T(2,128)S(1)} async-done(((f32[64,2,3,128]{3,1,2,0:T(2,128)}), f32[64,2,3,128]{3,1,2,0:T(2,128)S(1)}, u32[]{:S(2)}, u32[]{:S(2)}) %all-to-all-start.1) | async-done | bytes 196640 | tf_op jit(solution)/shard_map/all_to_all | solution.py:173
  (449 shorter events, 106.2 us)
Async XLA Ops:
  11.5 20.1 %copy-start = (f32[4,16,3,256]{3,1,2,0:T(8,128)S(1)}, f32[4,16,3,256]{3,1,2,0:T(8,128)}, u32[]{:S(2)}) copy-start(f32[4,16,3,256]{3,1,2,0:T(8,128)} %param.11) | copy-start | bytes 589828
  11.6 20.1 %copy-start.2 = (f32[4,16,256]{2,1,0:T(8,128)S(1)}, f32[4,16,256]{2,1,0:T(8,128)}, u32[]{:S(2)}) copy-start(f32[4,16,256]{2,1,0:T(8,128)} %param.13) | copy-start | bytes 196612
  11.6 20.1 %copy-start.3 = (f32[4,16,256]{2,1,0:T(8,128)S(1)}, f32[4,16,256]{2,1,0:T(8,128)}, u32[]{:S(2)}) copy-start(f32[4,16,256]{2,1,0:T(8,128)} %param.12) | copy-start | bytes 196612
  15.0 34.5 %all-to-all-start = ((f32[64,2,6,128]{3,1,2,0:T(2,128)}), f32[64,2,6,128]{3,1,2,0:T(2,128)S(1)}, u32[]{:S(2)}, u32[]{:S(2)}) async-start(f32[64,2,6,128]{3,1,2,0:T(2,128)} %copy.97), calls=%async_computation | async-start | bytes 786432 | tf_op jit(solution)/shard_map/all_to_all | solution.py:115
  31.6 99.5 %all-reduce.5.cloned.1.call-start = ((), (), s32[]{:S(2)}) async-start(), calls=%async_computation.2 | async-start | bytes 1089536 | tf_op jit(solution)/shard_map/psum | solution.py:155
  31.7 11.6 %collective-permute-start.1 = (f32[1,16,5,256]{3,1,0,2:T(8,128)S(1)}, f32[1,16,5,256]{3,1,0,2:T(8,128)S(1)}, u32[]{:S(2)}, u32[]{:S(2)}) collective-permute-start(f32[1,16,5,256]{3,1,0,2:T(8,128)S(1)} %get-tuple-element.304), channel_id=1, source_target_pairs={{8,0},{16,8},{24,16},{32,24},{40,32},{48,40},{56,48},{64,56},{72,6... | collective-permute-start | bytes 245768 | tf_op jit(solution)/shard_map/ppermute | solution.py:21
  33.0 10.3 %collective-permute-start = (f32[1,16,5,256]{3,1,0,2:T(8,128)S(1)}, f32[1,16,5,256]{3,1,0,2:T(8,128)S(1)}, u32[]{:S(2)}, u32[]{:S(2)}) collective-permute-start(f32[1,16,5,256]{3,1,0,2:T(8,128)S(1)} %get-tuple-element.303), channel_id=1, source_target_pairs={{0,8},{8,16},{16,24},{24,32},{32,40},{40,48},{48,56},{56,64},{64,7... | collective-permute-start | bytes 245768 | tf_op jit(solution)/shard_map/ppermute | solution.py:19
  43.3 53.0 %collective-permute-start.3 = (f32[6,1,5,256]{3,1,0,2:T(1,128)S(1)}, f32[6,1,5,256]{3,1,0,2:T(1,128)S(1)}, u32[]{:S(2)}, u32[]{:S(2)}) collective-permute-start(f32[6,1,5,256]{3,1,0,2:T(1,128)S(1)} %get-tuple-element.302), channel_id=1, source_target_pairs={{2,0},{4,2},{6,4},{3,1},{5,3},{7,5},{10,8},{12,10},{14,12},{11,9},... | collective-permute-start | bytes 92168 | tf_op jit(solution)/shard_map/ppermute | solution.py:21
  46.1 50.3 %collective-permute-start.2 = (f32[6,1,5,256]{3,1,0,2:T(1,128)S(1)}, f32[6,1,5,256]{3,1,0,2:T(1,128)S(1)}, u32[]{:S(2)}, u32[]{:S(2)}) collective-permute-start(f32[6,1,5,256]{3,1,0,2:T(1,128)S(1)} %get-tuple-element.301), channel_id=1, source_target_pairs={{0,2},{2,4},{4,6},{1,3},{3,5},{5,7},{8,10},{10,12},{12,14},{9,11},... | collective-permute-start | bytes 92168 | tf_op jit(solution)/shard_map/ppermute | solution.py:19
  131.1 8.2 %copy-start.1 = (f32[7,19,3,256]{3,2,1,0:T(4,128)S(1)}, f32[7,19,3,256]{3,2,1,0:T(4,128)}, u32[]{:S(2)}) copy-start(f32[7,19,3,256]{3,2,1,0:T(4,128)} %all-reduce.5.cloned.1.call-done) | copy-start | bytes 1225732
  132.2 7.1 %collective-permute-start.4 = (f32[2,19,3,256]{3,2,1,0:T(4,128)S(1)}, f32[2,19,3,256]{3,2,1,0:T(4,128)S(1)}, u32[]{:S(2)}, u32[]{:S(2)}) collective-permute-start(f32[2,19,3,256]{3,2,1,0:T(4,128)S(1)} %get-tuple-element.300), channel_id=1, source_target_pairs={{0,8},{8,16},{16,24},{24,32},{32,40},{40,48},{48,56},{56,64},{64,7... | collective-permute-start | bytes 350216 | tf_op jit(solution)/shard_map/ppermute | solution.py:19
  135.8 7.8 %collective-permute-start.5 = (f32[2,19,3,256]{3,2,1,0:T(4,128)S(1)}, f32[2,19,3,256]{3,2,1,0:T(4,128)S(1)}, u32[]{:S(2)}, u32[]{:S(2)}) collective-permute-start(f32[2,19,3,256]{3,2,1,0:T(4,128)S(1)} %get-tuple-element.299), channel_id=1, source_target_pairs={{8,0},{16,8},{24,16},{32,24},{40,32},{48,40},{56,48},{64,56},{72,6... | collective-permute-start | bytes 350216 | tf_op jit(solution)/shard_map/ppermute | solution.py:21
  143.7 4.9 %collective-permute-start.7 = (f32[11,2,3,256]{3,2,1,0:T(4,128)S(1)}, f32[11,2,3,256]{3,2,1,0:T(4,128)S(1)}, u32[]{:S(2)}, u32[]{:S(2)}) collective-permute-start(f32[11,2,3,256]{3,2,1,0:T(4,128)S(1)} %get-tuple-element.298), channel_id=1, source_target_pairs={{2,0},{4,2},{6,4},{3,1},{5,3},{7,5},{10,8},{12,10},{14,12},{11,9},... | collective-permute-start | bytes 202760 | tf_op jit(solution)/shard_map/ppermute | solution.py:21
  146.5 6.4 %collective-permute-start.6 = (f32[11,2,3,256]{3,2,1,0:T(4,128)S(1)}, f32[11,2,3,256]{3,2,1,0:T(4,128)S(1)}, u32[]{:S(2)}, u32[]{:S(2)}) collective-permute-start(f32[11,2,3,256]{3,2,1,0:T(4,128)S(1)} %get-tuple-element.297), channel_id=1, source_target_pairs={{0,2},{2,4},{4,6},{1,3},{3,5},{5,7},{8,10},{10,12},{12,14},{9,11},... | collective-permute-start | bytes 202760 | tf_op jit(solution)/shard_map/ppermute | solution.py:19
  148.1 5.0 %copy-start.5 = (pred[4]{0:T(512)(128)(4,1)S(1)}, pred[4]{0:T(512)(128)(4,1)}, u32[]{:S(2)}) copy-start(pred[4]{0:T(512)(128)(4,1)} %constant.173.clone.1) | copy-start | bytes 16
  153.1 0.7 copy-start.4
  154.3 6.2 %collective-permute-start.9 = (bf16[2,16,3,256]{3,2,1,0:T(4,128)(2,1)S(1)}, bf16[2,16,3,256]{3,2,1,0:T(4,128)(2,1)S(1)}, u32[]{:S(2)}, u32[]{:S(2)}) collective-permute-start(bf16[2,16,3,256]{3,2,1,0:T(4,128)(2,1)S(1)} %get-tuple-element.317), channel_id=1, source_target_pairs={{8,0},{16,8},{24,16},{32,24},{40,32},{48,40},{56,48},{64,56},{72,6... | collective-permute-start | bytes 147464 | tf_op jit(solution)/shard_map/ppermute | solution.py:21
  155.6 6.4 %collective-permute-start.8 = (bf16[2,16,3,256]{3,2,1,0:T(4,128)(2,1)S(1)}, bf16[2,16,3,256]{3,2,1,0:T(4,128)(2,1)S(1)}, u32[]{:S(2)}, u32[]{:S(2)}) collective-permute-start(bf16[2,16,3,256]{3,2,1,0:T(4,128)(2,1)S(1)} %get-tuple-element.316), channel_id=1, source_target_pairs={{0,8},{8,16},{16,24},{24,32},{32,40},{40,48},{48,56},{56,64},{64,7... | collective-permute-start | bytes 147464 | tf_op jit(solution)/shard_map/ppermute | solution.py:19
  162.1 4.0 %collective-permute-start.11 = (bf16[8,2,3,256]{3,2,1,0:T(4,128)(2,1)S(1)}, bf16[8,2,3,256]{3,2,1,0:T(4,128)(2,1)S(1)}, u32[]{:S(2)}, u32[]{:S(2)}) collective-permute-start(bf16[8,2,3,256]{3,2,1,0:T(4,128)(2,1)S(1)} %get-tuple-element.306), channel_id=1, source_target_pairs={{2,0},{4,2},{6,4},{3,1},{5,3},{7,5},{10,8},{12,10},{14,12},{11,9},... | collective-permute-start | bytes 73736 | tf_op jit(solution)/shard_map/ppermute | solution.py:21
  164.6 5.8 %collective-permute-start.10 = (bf16[8,2,3,256]{3,2,1,0:T(4,128)(2,1)S(1)}, bf16[8,2,3,256]{3,2,1,0:T(4,128)(2,1)S(1)}, u32[]{:S(2)}, u32[]{:S(2)}) collective-permute-start(bf16[8,2,3,256]{3,2,1,0:T(4,128)(2,1)S(1)} %get-tuple-element.305), channel_id=1, source_target_pairs={{0,2},{2,4},{4,6},{1,3},{3,5},{5,7},{8,10},{10,12},{12,14},{9,11},... | collective-permute-start | bytes 73736 | tf_op jit(solution)/shard_map/ppermute | solution.py:19
  218.8 32.4 %all-to-all-start.1 = ((f32[64,2,3,128]{3,1,2,0:T(2,128)}), f32[64,2,3,128]{3,1,2,0:T(2,128)S(1)}, u32[]{:S(2)}, u32[]{:S(2)}) async-start(f32[64,2,3,128]{3,1,2,0:T(2,128)} %copy.103), calls=%async_computation.1 | async-start | bytes 393216 | tf_op jit(solution)/shard_map/all_to_all | solution.py:173
Sparse Core Ops, SparseCore 0:
  96.5 34.5 all-reduce.4
where the time goes:
time: 260 us; the launch traced here: 259 us
  waiting for transfers between devices  71.7 us (28%)
  starting transfers between devices  64.1 us (25%)
  other arithmetic  48.4 us (19%)
  matrix products  37.3 us (14%)
  local copies, waits for them, and re-layouts  20.7 us (8%)
  between operations  14.5 us (6%)
  loops' own time  2.82 us (1%)
    psum x1, waiting for transfers between devices, body(): total_force = lax.psum(spread_pad, 'struct')  34 us
    select_n x80, other arithmetic, kernel_weight(): return jnp.where(distance < 1.0, inner, outer)  29.9 us
    dot_general x16, matrix products, sample_turn(): lax.dot_general(flat_field, depth_weight, (((1,), (2,)), ((), ())), prefe...  25.9 us
    all_to_all x1, starting transfers between devices, body(): lax.all_to_all(sampled, 'fluid', split_axis=0, concat_axis=0, tiled=True)  19.2 us
    all_to_all x1, starting transfers between devices, body(): lax.all_to_all(outgoing.reshape(slabs, capacity, 6, markers), 'fluid', sp...  16.6 us
    ppermute x6, starting transfers between devices, with_halo(): lax.ppermute(tail, axis, [(i, (i + 1) % count) for i in range(ends)])  16.4 us
    all_to_all x1, waiting for transfers between devices, body(): lax.all_to_all(sampled, 'fluid', split_axis=0, concat_axis=0, tiled=True)  12.4 us
    ppermute x6, waiting for transfers between devices, with_halo(): lax.ppermute(tail, axis, [(i, (i + 1) % count) for i in range(ends)])  12.3 us
  transfers between devices with their start and end apart: 15, of which 12 were waited for; matrix products, arithmetic and copies ran while one was open for 18% of the time, Pallas kernels for 0%

commit v1 on v0

v1 whole, which is shorter than its diff:
```python
import math

import jax
import jax.numpy as jnp
from jax import lax
from jax.experimental import pallas as pl
from jax.experimental.pallas import tpu as pltpu
from jax.sharding import PartitionSpec as P

M = 128
NZ = 256
YP = 24
XE = 7
ROWS = XE * 3 * YP
ROWS_PAD = 512
GROUP = 8
PAIR = 2

VMEM = pl.BlockSpec(memory_space=pltpu.VMEM)
SMEM = pl.BlockSpec(memory_space=pltpu.SMEM)


def iota(shape, dim):
    return lax.broadcasted_iota(jnp.int32, shape, dim)


def pack_kernel(blocks, slab_ref, offset_ref, base_ref, force_ref, out_ref, pos_ref, count, coords):
    slots = out_ref.shape[0] // 6
    out_ref[...] = jnp.zeros_like(out_ref)
    coords[...] = base_ref[...].astype(jnp.float32) + offset_ref[...]

    def clear(i, carry):
        count[i] = 0
        return carry

    lax.fori_loop(0, slots // 2, clear, 0)
    for b in range(blocks):
        slab = slab_ref[b]
        place = count[slab]
        count[slab] = place + 1
        slot = slab * 2 + place
        pos_ref[b] = slot
        for j in range(3):
            out_ref[pl.ds(slot * 6 + j, 1), :] = coords[j, b : b + 1, :]
            out_ref[pl.ds(slot * 6 + 3 + j, 1), :] = force_ref[j, b : b + 1, :]


def prepare_weights(load_ref, base_ref, weight_ref):
    rows = load_ref.shape[0]
    step = math.gcd(rows, 64)

    def turn(i, carry):
        at = pl.ds(pl.multiple_of(i * step, step), step)
        place = load_ref[at, :]
        base = jnp.floor(place)
        part = place - base
        root = jnp.sqrt(1.0 + 4.0 * part * (1.0 - part)) * 0.125
        falling = (3.0 - 2.0 * part) * 0.125
        rising = (1.0 + 2.0 * part) * 0.125
        base_ref[at, :] = base.astype(jnp.int32)
        weight_ref[0, at, :] = falling - root
        weight_ref[1, at, :] = falling + root
        weight_ref[2, at, :] = rising + root
        weight_ref[3, at, :] = rising - root
        return carry

    lax.fori_loop(0, rows // step, turn, 0)


def pick(index, weights):
    out = jnp.where(index == 0, weights[0], 0.0)
    for j in range(1, 4):
        out = jnp.where(index == j, weights[j], out)
    return out


def row8(ref, row):
    return jnp.broadcast_to(ref[pl.ds(row, 1), :], (8, M))


def block_weights(base_ref, weight_ref, row, row_x):
    sub = iota((8, M), 0)
    bx = row8(base_ref, row)
    by = row8(base_ref, row + 1)
    bz = row8(base_ref, row + 2)
    wx_in = [row8(weight_ref.at[j], row) for j in range(4)]
    wy_in = [row8(weight_ref.at[j], row + 1) for j in range(4)]
    wz_in = [row8(weight_ref.at[j], row + 2) for j in range(4)]
    row_x[...] = pick(sub - bx, wx_in)
    along_x = [jnp.broadcast_to(row_x[x : x + 1, :], (8, M)) for x in range(XE)]
    cells_y = [
        sub,
        sub + 8,
        jnp.where(sub < 2, sub + 16, jnp.where(sub == 7, -1, -100)),
    ]
    along_y = [pick(cell - by + 1, wy_in) for cell in cells_y]
    lead = sub - bz + 1
    tile = (7 - lead) >> 3
    value = pick(lead & 7, wz_in)
    along_z = jnp.concatenate(
        [jnp.where(tile == r, value, 0.0) for r in range(NZ // 8)], axis=0
    ).astype(jnp.bfloat16)
    return along_x, along_y, along_z


def spread_kernel(load_ref, out_ref, base_ref, weight_ref, row_x, left, right, total):
    blocks = load_ref.shape[0] // 6
    prepare_weights(load_ref, base_ref, weight_ref)
    total[...] = jnp.zeros_like(total)

    def turn(i, carry):
        for g in range(GROUP):
            row = (i * GROUP + g) * 6
            along_x, along_y, along_z = block_weights(base_ref, weight_ref, row, row_x.at[g])
            right[:, g * M : (g + 1) * M] = along_z
            force = [row8(load_ref, row + 3 + c) for c in range(3)]
            tiles = []
            for x in range(XE):
                for c in range(3):
                    push = along_x[x] * force[c]
                    tiles += [push * along_y[k] for k in range(3)]
            tiles.append(jnp.zeros((8, M), jnp.float32))
            left[:, g * M : (g + 1) * M] = jnp.concatenate(tiles, axis=0).astype(jnp.bfloat16)
        total[...] += lax.dot_general(
            left[...], right[...], (((1,), (1,)), ((), ())), preferred_element_type=jnp.float32
        )
        return carry

    lax.fori_loop(0, blocks // GROUP, turn, 0)
    out_ref[...] = total[...].astype(out_ref.dtype)


def join_kernel(mine_ref, other_ref, old_ref, sum_ref, low_ref, high_ref):
    rim = 9 * YP
    sum_ref[...] = 0.5 * (
        mine_ref[0:ROWS, :].astype(jnp.float32) + other_ref[0:ROWS, :].astype(jnp.float32)
    )
    for x in range(4):
        for c in range(3):
            at = ((x + 1) * 3 + c) * YP
            sum_ref[at : at + 16, :] += old_ref[x, c]
    low_ref[...] = sum_ref[0:rim, :].astype(jnp.bfloat16)
    high_ref[...] = sum_ref[ROWS - rim : ROWS, :].astype(jnp.bfloat16)


HIGH_ROWS = (15, 16, 17)
LOW_ROWS = (23, 0, 1)


def fold_kernel(sum_ref, left_ref, right_ref, out_ref, low_ref, high_ref, low, high):
    rim = 9 * YP
    out_ref[rim : ROWS - rim, :] = sum_ref[rim : ROWS - rim, :]
    out_ref[0:rim, :] = sum_ref[0:rim, :] + left_ref[...].astype(jnp.float32)
    out_ref[ROWS - rim : ROWS, :] = sum_ref[ROWS - rim : ROWS, :] + right_ref[...].astype(jnp.float32)
    low[...] = jnp.zeros_like(low)
    high[...] = jnp.zeros_like(high)
    for g in range(XE * 3):
        for j in range(3):
            lanes = slice(j * NZ, (j + 1) * NZ)
            low[g : g + 1, lanes] = out_ref[g * YP + LOW_ROWS[j] : g * YP + LOW_ROWS[j] + 1, :]
            high[g : g + 1, lanes] = out_ref[g * YP + HIGH_ROWS[j] : g * YP + HIGH_ROWS[j] + 1, :]
    low_ref[...] = low[...].astype(jnp.bfloat16)
    high_ref[...] = high[...].astype(jnp.bfloat16)


def sample_kernel(
    fluid_count,
    sub_count,
    place_ref,
    load_ref,
    sum_ref,
    below_ref,
    above_ref,
    fresh_ref,
    out_ref,
    base_ref,
    weight_ref,
    row_x,
    grid,
    field,
    below,
    above,
):
    blocks = load_ref.shape[0] // 6
    prepare_weights(load_ref, base_ref, weight_ref)
    grid[...] = sum_ref[...]
    below[...] = below_ref[...].astype(jnp.float32)
    above[...] = above_ref[...].astype(jnp.float32)
    for g in range(XE * 3):
        for j in range(3):
            lanes = slice(j * NZ, (j + 1) * NZ)
            at = g * YP + LOW_ROWS[j]
            grid[at : at + 1, :] += below[g : g + 1, lanes]
            at = g * YP + HIGH_ROWS[j]
            grid[at : at + 1, :] += above[g : g + 1, lanes]
    for x in range(4):
        for c in range(3):
            at = ((x + 1) * 3 + c) * YP
            fresh_ref[x, c] = grid[at : at + 16, :]
    first = place_ref[0]
    second = place_ref[1]
    sub = iota((8, NZ), 0)
    inside = ((sub < 2) & (second < sub_count - 1)) | ((sub == 7) & (second > 0))
    for g in range(XE * 3):
        at = g * YP + 16
        grid[at : at + 8, :] = jnp.where(inside, grid[at : at + 8, :], 0.0)
    rim = 3 * YP

    @pl.when(first == 0)
    def _():
        grid[0:rim, :] = jnp.zeros((rim, NZ), jnp.float32)

    @pl.when(first == fluid_count - 1)
    def _():
        grid[5 * rim : ROWS, :] = jnp.zeros((2 * rim, NZ), jnp.float32)

    field[0:ROWS, :] = grid[...].astype(jnp.bfloat16)
    field[ROWS:ROWS_PAD, :] = jnp.zeros((ROWS_PAD - ROWS, NZ), jnp.bfloat16)

    def turn(i, carry):
        parts = []
        zs = []
        for g in range(PAIR):
            row = (i * PAIR + g) * 6
            along_x, along_y, along_z = block_weights(base_ref, weight_ref, row, row_x.at[g])
            parts.append((along_x, along_y))
            zs.append(along_z)
        seen = lax.dot_general(
            field[...],
            jnp.concatenate(zs, axis=1),
            (((1,), (0,)), ((), ())),
            preferred_element_type=jnp.float32,
        )
        for g in range(PAIR):
            along_x, along_y = parts[g]
            sums = [jnp.zeros((8, M), jnp.float32) for _ in range(3)]
            for x in range(XE):
                for k in range(3):
                    plane = along_x[x] * along_y[k]
                    for c in range(3):
                        at = (x * 3 + c) * YP + k * 8
                        sums[c] = sums[c] + plane * seen[at : at + 8, g * M : (g + 1) * M]
            for c in range(3):
                out_ref[pl.ds((i * PAIR + g) * 3 + c, 1), :] = jnp.sum(
                    sums[c], axis=0, keepdims=True
                )
        return carry

    lax.fori_loop(0, blocks // PAIR, turn, 0)


def take_kernel(blocks, pos_ref, in_ref, out_ref):
    for b in range(blocks):
        slot = pos_ref[b]
        for c in range(3):
            out_ref[c, b : b + 1, :] = in_ref[pl.ds(slot * 3 + c, 1), :]


def shift(array, axis, by):
    count = lax.axis_size(axis)
    if by > 0:
        pairs = [(i, i + 1) for i in range(count - 1)]
    else:
        pairs = [(i + 1, i) for i in range(count - 1)]
    return lax.ppermute(array, axis, pairs)


def old_part(velocity, pressure, viscosity):
    v = jnp.transpose(velocity, (0, 2, 1, 3))
    p = pressure[:, None]
    n = viscosity[:, None]
    every = jnp.concatenate([v, p, n], axis=1)
    before_x = shift(every[-1:], "fluid", 1)
    after_x = shift(every[:1], "fluid", -1)
    before_y = shift(every[:, :, -1:], "sub", 1)
    after_y = shift(every[:, :, :1], "sub", -1)
    zero = jnp.zeros_like(every[..., :1])
    around = (
        jnp.concatenate([every[1:], after_x], axis=0),
        jnp.concatenate([before_x, every[:-1]], axis=0),
        jnp.concatenate([every[:, :, 1:], after_y], axis=2),
        jnp.concatenate([before_y, every[:, :, :-1]], axis=2),
        jnp.concatenate([every[..., 1:], zero], axis=3),
        jnp.concatenate([zero, every[..., :-1]], axis=3),
    )
    viscous = jnp.zeros_like(v)
    for near in around:
        viscous = viscous + 0.5 * (n + near[:, 4:5]) * (near[:, 0:3] - v)
    gradient = jnp.concatenate([around[k][:, 3:4] - p for k in (0, 2, 4)], axis=1)
    return v + 0.5 * (viscous - gradient)


def kernel_params():
    return pltpu.CompilerParams(vmem_limit_bytes=60 * 1024 * 1024)


def body(velocity, pressure, viscosity, marker_force, marker_offset, cell_base, block_slab):
    f32, bf16 = jnp.float32, jnp.bfloat16
    shape = jax.ShapeDtypeStruct
    blocks = marker_force.shape[0]
    slabs = lax.axis_size("fluid")
    subs = lax.axis_size("sub")
    slots = 2 * slabs
    swap01 = lambda array: jnp.transpose(array, (1, 0, 2))
    payload, position = pl.pallas_call(
        lambda *refs: pack_kernel(blocks, *refs),
        out_shape=(shape((slots * 6, M), f32), shape((blocks,), jnp.int32)),
        in_specs=[SMEM, VMEM, VMEM, VMEM],
        out_specs=(VMEM, SMEM),
        scratch_shapes=[pltpu.SMEM((slabs,), jnp.int32), pltpu.VMEM((3, blocks, M), f32)],
        name="pack",
    )(block_slab[:, 0], swap01(marker_offset), swap01(cell_base), swap01(marker_force))
    arrived = lax.all_to_all(
        payload.reshape(slabs, 3, 4, M), "fluid", split_axis=0, concat_axis=0, tiled=True
    ).reshape(slots * 6, M)
    old = old_part(velocity, pressure, viscosity)
    partial_grid = pl.pallas_call(
        spread_kernel,
        out_shape=shape((ROWS_PAD, NZ), bf16),
        in_specs=[VMEM],
        out_specs=VMEM,
        scratch_shapes=[
            pltpu.VMEM((slots * 6, M), jnp.int32),
            pltpu.VMEM((4, slots * 6, M), f32),
            pltpu.VMEM((GROUP, 8, M), f32),
            pltpu.VMEM((ROWS_PAD, GROUP * M), bf16),
            pltpu.VMEM((NZ, GROUP * M), bf16),
            pltpu.VMEM((ROWS_PAD, NZ), f32),
        ],
        compiler_params=kernel_params(),
        name="spread",
    )(arrived)
    other_grid = lax.ppermute(partial_grid, "struct", [(0, 1), (1, 0)])
    rim = 9 * YP
    summed, low, high = pl.pallas_call(
        join_kernel,
        out_shape=(shape((ROWS, NZ), f32), shape((rim, NZ), bf16), shape((rim, NZ), bf16)),
        in_specs=[VMEM] * 3,
        out_specs=(VMEM,) * 3,
        name="join",
    )(partial_grid, other_grid, old)
    from_left = shift(high, "fluid", 1)
    from_right = shift(low, "fluid", -1)
    folded, low, high = pl.pallas_call(
        fold_kernel,
        out_shape=(shape((ROWS, NZ), f32), shape((24, 3 * NZ), bf16), shape((24, 3 * NZ), bf16)),
        in_specs=[VMEM] * 3,
        out_specs=(VMEM,) * 3,
        scratch_shapes=[pltpu.VMEM((24, 3 * NZ), f32)] * 2,
        name="fold",
    )(summed, from_left, from_right)
    from_below = shift(high, "sub", 1)
    from_above = shift(low, "sub", -1)
    place = jnp.stack([lax.axis_index("fluid"), lax.axis_index("sub")]).astype(jnp.int32)
    fresh, sampled = pl.pallas_call(
        lambda *refs: sample_kernel(slabs, subs, *refs),
        out_shape=(shape((4, 3, 16, NZ), f32), shape((slots * 3, M), f32)),
        in_specs=[SMEM] + [VMEM] * 4,
        out_specs=(VMEM, VMEM),
        scratch_shapes=[
            pltpu.VMEM((slots * 6, M), jnp.int32),
            pltpu.VMEM((4, slots * 6, M), f32),
            pltpu.VMEM((PAIR, 8, M), f32),
            pltpu.VMEM((ROWS, NZ), f32),
            pltpu.VMEM((ROWS_PAD, NZ), bf16),
            pltpu.VMEM((24, 3 * NZ), f32),
            pltpu.VMEM((24, 3 * NZ), f32),
        ],
        compiler_params=kernel_params(),
        name="sample",
    )(place, arrived, folded, from_below, from_above)
    returned = lax.all_to_all(
        sampled.reshape(slabs, 3, 2, M), "fluid", split_axis=0, concat_axis=0, tiled=True
    ).reshape(slots * 3, M)
    result = pl.pallas_call(
        lambda *refs: take_kernel(blocks, *refs),
        out_shape=shape((3, blocks, M), f32),
        in_specs=[SMEM, VMEM],
        out_specs=VMEM,
        name="take",
    )(position, returned)
    return (jnp.transpose(fresh, (0, 2, 1, 3)), swap01(result))


def solution(mesh):
    return jax.shard_map(
        body,
        mesh=mesh,
        in_specs=(
            P("fluid", "sub", None, None),
            P("fluid", "sub", None),
            P("fluid", "sub", None),
            P(("fluid", "sub", "struct"), None, None),
            P(("fluid", "sub", "struct"), None, None),
            P(("fluid", "sub", "struct"), None, None),
            P(("fluid", "sub", "struct"), None),
        ),
        out_specs=(P("fluid", "sub", None, None), P(("fluid", "sub", "struct"), None, None)),
        check_vma=False,
    )
```

time: 260 us -> 130 us (0.50)
  waiting for transfers between devices: 71.7 us -> 19.9 us
  other arithmetic: 48.4 us -> 2.73 us
  Pallas kernels: 0 us -> 40 us
  matrix products: 37.3 us -> 0 us
  starting transfers between devices: 64.1 us -> 38.7 us
  blocking collectives: 0 us -> 22.2 us
  local copies, waits for them, and re-layouts: 20.7 us -> 3 us
  between operations: 14.5 us -> 0.86 us
  loops' own time: 2.82 us -> 0 us
    pallas_call x0 -> x6, Pallas kernels: none -> 40 us  [the longest x1 18.8 us: body(): pl.pallas_call(lambda *refs: sample_kernel(slabs, subs, *refs), out_shape...]
    dot_general x32 -> x0, matrix products: 37.3 us -> none  [the longest x16 25.9 us: sample_turn(): lax.dot_general(flat_field, depth_weight, (((1,), (2,)), ((), ())), prefe...]
    psum x1 -> x0, waiting for transfers between devices: 34 us -> none  [body(): total_force = lax.psum(spread_pad, 'struct')]
    select_n x81 -> x0, other arithmetic: 30.6 us -> none  [the longest x80 29.9 us: kernel_weight(): return jnp.where(distance < 1.0, inner, outer)]
    all_to_all x0 -> x1, blocking collectives: none -> 22.2 us  [body(): lax.all_to_all(sampled.reshape(slabs, 3, 2, M), 'fluid', split_axis=0, co...]
    all_to_all x2 -> x1, starting transfers between devices: 35.8 us -> 16.7 us  [body(): lax.all_to_all(payload.reshape(slabs, 3, 4, M), 'fluid', split_axis=0, co...]
    ppermute x12 -> x9, waiting for transfers between devices: 23.1 us -> 7.54 us  [the longest x8 6.9 us: shift(): return lax.ppermute(array, axis, pairs)]
    while x32 -> x0, local copies, waits for them, and re-layouts: 10 us -> none
  transfers between devices with their start and end apart: 15 -> 10, of which waited for: 12 -> 5; matrix products, arithmetic and copies ran while one was open for 18% -> 2% of each run, Pallas kernels for 0% -> 12%
where the time goes in v1:
time: 130 us; the launch traced here: 127 us
  Pallas kernels  40 us (31%)
  starting transfers between devices  38.7 us (30%)
  blocking collectives  22.2 us (17%)
  waiting for transfers between devices  19.9 us (15%)
  local copies, waits for them, and re-layouts  3 us (2%)
  other arithmetic  2.73 us (2%)
    all_to_all x1, blocking collectives, body(): lax.all_to_all(sampled.reshape(slabs, 3, 2, M), 'fluid', split_axis=0, co...  22.2 us
    ppermute x8, starting transfers between devices, shift(): return lax.ppermute(array, axis, pairs)  20.1 us
    pallas_call x1, Pallas kernels, body(): pl.pallas_call(lambda *refs: sample_kernel(slabs, subs, *refs), out_shape...  18.8 us
    all_to_all x1, starting transfers between devices, body(): lax.all_to_all(payload.reshape(slabs, 3, 4, M), 'fluid', split_axis=0, co...  16.7 us
    pallas_call x1, Pallas kernels, body(): pl.pallas_call(spread_kernel, out_shape=shape((ROWS_PAD, NZ), bf16), in_s...  13 us
    all_to_all x1, waiting for transfers between devices, body(): lax.all_to_all(payload.reshape(slabs, 3, 4, M), 'fluid', split_axis=0, co...  12.3 us
    ppermute x8, waiting for transfers between devices, shift(): return lax.ppermute(array, axis, pairs)  6.9 us
    unnamed x18, local copies, waits for them, and re-layouts  2.74 us
  transfers between devices with their start and end apart: 10, of which 5 were waited for; matrix products, arithmetic and copies ran while one was open for 2% of the time, Pallas kernels for 12%

profile of v1, /device:TPU:6, one launch (start us, length us, event | category | flops | bytes accessed | tf_op | source)
XLA Modules:
  0.0 127.4 jit_solution(13678572561922185146)
XLA Ops:
  0.6 1.0 pad_maximum_fusion
  1.7 1.3 %collective-permute-start.1 = (f32[1,5,16,256]{3,2,1,0:T(8,128)S(1)}, f32[1,5,16,256]{3,2,1,0:T(8,128)S(1)}, u32[]{:S(2)}, u32[]{:S(2)}) collective-permute-start(f32[1,5,16,256]{3,2,1,0:T(8,128)S(1)} %get-tuple-element.29), channel_id=1, source_target_pairs={{8,0},{16,8},{24,16},{32,24},{40,32},{48,40},{56,48},{64,56},{72,6... | collective-permute-start | bytes 245768 | tf_op jit(solution)/shard_map/ppermute | solution.py:265
  3.0 4.6 %collective-permute-start.2 = (f32[1,5,16,256]{3,2,1,0:T(8,128)S(1)}, f32[1,5,16,256]{3,2,1,0:T(8,128)S(1)}, u32[]{:S(2)}, u32[]{:S(2)}) collective-permute-start(f32[1,5,16,256]{3,2,1,0:T(8,128)S(1)} %get-tuple-element.28), channel_id=1, source_target_pairs={{0,8},{8,16},{16,24},{24,32},{32,40},{40,48},{48,56},{56,64},{64,7... | collective-permute-start | bytes 245768 | tf_op jit(solution)/shard_map/ppermute | solution.py:265
  7.5 2.5 %pack.1 = (f32[768,128]{1,0:T(8,128)}, s32[64]{0:T(128)}) custom-call(s32[64]{0:T(128)} %bitcast.52, f32[3,64,128]{2,1,0:T(8,128)} %bitcast.48, s32[3,64,128]{2,1,0:T(8,128)} %bitcast.49, f32[3,64,128]{2,1,0:T(8,128)} %bitcast.50), custom_call_target="tpu_custom_call" | custom-call | tf_op jit(solution)/shard_map/pack/pallas_call | solution.py:305
  10.1 16.7 %all-to-all-start = ((f32[64,3,4,128]{3,2,1,0:T(4,128)}), f32[64,3,4,128]{3,2,1,0:T(4,128)S(1)}, u32[]{:S(2)}, u32[]{:S(2)}) async-start(f32[64,3,4,128]{3,2,1,0:T(4,128)} %bitcast.46), calls=%async_computation | async-start | bytes 786432 | tf_op jit(solution)/shard_map/all_to_all | solution.py:313
  26.9 2.7 %collective-permute-start.3 = (f32[4,5,1,256]{3,2,1,0:T(1,128)S(1)}, f32[4,5,1,256]{3,2,1,0:T(1,128)S(1)}, u32[]{:S(2)}, u32[]{:S(2)}) collective-permute-start(f32[4,5,1,256]{3,2,1,0:T(1,128)S(1)} %get-tuple-element.33), channel_id=1, source_target_pairs={{2,0},{4,2},{6,4},{3,1},{5,3},{7,5},{10,8},{12,10},{14,12},{11,9},... | collective-permute-start | bytes 61448 | tf_op jit(solution)/shard_map/ppermute | solution.py:265
  29.6 1.3 %collective-permute-start.4 = (f32[4,5,1,256]{3,2,1,0:T(1,128)S(1)}, f32[4,5,1,256]{3,2,1,0:T(1,128)S(1)}, u32[]{:S(2)}, u32[]{:S(2)}) collective-permute-start(f32[4,5,1,256]{3,2,1,0:T(1,128)S(1)} %get-tuple-element.32), channel_id=1, source_target_pairs={{0,2},{2,4},{4,6},{1,3},{3,5},{5,7},{8,10},{10,12},{12,14},{9,11},... | collective-permute-start | bytes 61448 | tf_op jit(solution)/shard_map/ppermute | solution.py:265
  31.2 12.3 %all-to-all-done = f32[64,3,4,128]{3,2,1,0:T(4,128)S(1)} async-done(((f32[64,3,4,128]{3,2,1,0:T(4,128)}), f32[64,3,4,128]{3,2,1,0:T(4,128)S(1)}, u32[]{:S(2)}, u32[]{:S(2)}) %all-to-all-start) | async-done | bytes 393248 | tf_op jit(solution)/shard_map/all_to_all | solution.py:313
  43.5 0.8 copy-done
  44.3 13.0 %spread.1.mine_ref = bf16[512,256]{1,0:T(8,128)(2,1)} custom-call(f32[768,128]{1,0:T(8,128)} %bitcast.37), custom_call_target="tpu_custom_call" | custom-call | tf_op jit(solution)/shard_map/spread/pallas_call | solution.py:317
  57.3 1.9 %collective-permute-start = (bf16[512,256]{1,0:T(8,128)(2,1)}, bf16[512,256]{1,0:T(8,128)(2,1)S(1)}, u32[]{:S(2)}, u32[]{:S(2)}) collective-permute-start(bf16[512,256]{1,0:T(8,128)(2,1)} %spread.1.mine_ref), channel_id=1, source_target_pairs={{0,1},{1,0},{2,3},{3,2},{4,5},{5,4},{6,7},{7,6},{8,9},{9,8},{10,11... | collective-permute-start | bytes 786440 | tf_op jit(solution)/shard_map/ppermute | solution.py:333
  59.4 0.9 fusion.6.old_ref
  61.6 2.0 %join.1 = (f32[504,256]{1,0:T(8,128)}, bf16[216,256]{1,0:T(8,128)(2,1)}, bf16[216,256]{1,0:T(8,128)(2,1)}) custom-call(bf16[512,256]{1,0:T(8,128)(2,1)} %spread.1.mine_ref, bf16[512,256]{1,0:T(8,128)(2,1)} %copy-done.4, f32[4,3,16,256]{3,2,1,0:T(8,128)} %fusion.6.old_ref), custom_call_target="tpu_custom_call" | custom-call | tf_op jit(solution)/shard_map/join/pallas_call | solution.py:335
  63.7 3.1 %collective-permute-start.5 = (bf16[216,256]{1,0:T(8,128)(2,1)}, bf16[216,256]{1,0:T(8,128)(2,1)S(1)}, u32[]{:S(2)}, u32[]{:S(2)}) collective-permute-start(bf16[216,256]{1,0:T(8,128)(2,1)} %get-tuple-element.14), channel_id=1, source_target_pairs={{0,8},{8,16},{16,24},{24,32},{32,40},{40,48},{48,56},{56,64},{64,7... | collective-permute-start | bytes 331784 | tf_op jit(solution)/shard_map/ppermute | solution.py:265
  66.8 1.3 %collective-permute-start.6 = (bf16[216,256]{1,0:T(8,128)(2,1)}, bf16[216,256]{1,0:T(8,128)(2,1)S(1)}, u32[]{:S(2)}, u32[]{:S(2)}) collective-permute-start(bf16[216,256]{1,0:T(8,128)(2,1)} %get-tuple-element.15), channel_id=1, source_target_pairs={{8,0},{16,8},{24,16},{32,24},{40,32},{48,40},{56,48},{64,56},{72,6... | collective-permute-start | bytes 331784 | tf_op jit(solution)/shard_map/ppermute | solution.py:265
  68.1 1.6 %collective-permute-done.5.left_ref = bf16[216,256]{1,0:T(8,128)(2,1)S(1)} collective-permute-done((bf16[216,256]{1,0:T(8,128)(2,1)}, bf16[216,256]{1,0:T(8,128)(2,1)S(1)}, u32[]{:S(2)}, u32[]{:S(2)}) %collective-permute-start.5) | collective-permute-done | bytes 110624 | tf_op jit(solution)/shard_map/ppermute | solution.py:265
  69.7 4.0 %collective-permute-done.6.right_ref = bf16[216,256]{1,0:T(8,128)(2,1)S(1)} collective-permute-done((bf16[216,256]{1,0:T(8,128)(2,1)}, bf16[216,256]{1,0:T(8,128)(2,1)S(1)}, u32[]{:S(2)}, u32[]{:S(2)}) %collective-permute-start.6) | collective-permute-done | bytes 110624 | tf_op jit(solution)/shard_map/ppermute | solution.py:265
  74.3 2.0 %fold.1 = (f32[504,256]{1,0:T(8,128)}, bf16[24,768]{1,0:T(8,128)(2,1)}, bf16[24,768]{1,0:T(8,128)(2,1)}) custom-call(f32[504,256]{1,0:T(8,128)} %get-tuple-element.13.sum_ref, bf16[216,256]{1,0:T(8,128)(2,1)} %copy-done.5, bf16[216,256]{1,0:T(8,128)(2,1)} %copy-done.6), custom_call_target="tpu_custom_call" | custom-call | tf_op jit(solution)/shard_map/fold/pallas_call | solution.py:344
  76.3 1.3 %collective-permute-start.7 = (bf16[24,768]{1,0:T(8,128)(2,1)}, bf16[24,768]{1,0:T(8,128)(2,1)S(1)}, u32[]{:S(2)}, u32[]{:S(2)}) collective-permute-start(bf16[24,768]{1,0:T(8,128)(2,1)} %get-tuple-element.17), channel_id=1, source_target_pairs={{0,2},{2,4},{4,6},{1,3},{3,5},{5,7},{8,10},{10,12},{12,14},{9,11},... | collective-permute-start | bytes 110600 | tf_op jit(solution)/shard_map/ppermute | solution.py:265
  77.6 4.5 %collective-permute-start.8 = (bf16[24,768]{1,0:T(8,128)(2,1)}, bf16[24,768]{1,0:T(8,128)(2,1)S(1)}, u32[]{:S(2)}, u32[]{:S(2)}) collective-permute-start(bf16[24,768]{1,0:T(8,128)(2,1)} %get-tuple-element.18), channel_id=1, source_target_pairs={{2,0},{4,2},{6,4},{3,1},{5,3},{7,5},{10,8},{12,10},{14,12},{11,9},... | collective-permute-start | bytes 110600 | tf_op jit(solution)/shard_map/ppermute | solution.py:265
  82.8 1.3 collective-permute-done.8.refs_4_
  84.7 18.8 %sample.1 = (f32[4,3,16,256]{3,2,1,0:T(8,128)}, f32[384,128]{1,0:T(8,128)}) custom-call(s32[2]{0:T(128)} %pad_add_fusion.refs_0_, f32[768,128]{1,0:T(8,128)} %bitcast.38, f32[504,256]{1,0:T(8,128)} %get-tuple-element.16.refs_2_, bf16[24,768]{1,0:T(8,128)(2,1)} %copy-done.7, bf16[24,768]{1,0:T(8,128)(2,1)} %copy-done.8), custom_call_target="tpu_custom_call" | custom-call | tf_op jit(solution)/shard_map/sample/pallas_call | solution.py:355
  103.5 22.2 %all_to_all.10 = f32[64,3,2,128]{3,2,1,0:T(2,128)} all-to-all(f32[64,3,2,128]{3,2,1,0:T(2,128)} %bitcast.47), channel_id=1, replica_groups=mesh['fluid'=64,'sub'=4,'struct'=2] {'fluid'}, dimensions={0} | all-to-all | bytes 393216 | tf_op jit(solution)/shard_map/all_to_all | solution.py:372
  125.7 1.7 %take.1 = f32[3,64,128]{2,1,0:T(8,128)} custom-call(s32[64]{0:T(128)} %get-tuple-element.20.refs_0_, f32[384,128]{1,0:T(8,128)} %bitcast.41), custom_call_target="tpu_custom_call" | custom-call | tf_op jit(solution)/shard_map/take/pallas_call | solution.py:375
  (30 shorter events, 3.7 us)
Async XLA Ops:
  1.7 57.6 %collective-permute-start.1 = (f32[1,5,16,256]{3,2,1,0:T(8,128)S(1)}, f32[1,5,16,256]{3,2,1,0:T(8,128)S(1)}, u32[]{:S(2)}, u32[]{:S(2)}) collective-permute-start(f32[1,5,16,256]{3,2,1,0:T(8,128)S(1)} %get-tuple-element.29), channel_id=1, source_target_pairs={{8,0},{16,8},{24,16},{32,24},{40,32},{48,40},{56,48},{64,56},{72,6... | collective-permute-start | bytes 245768 | tf_op jit(solution)/shard_map/ppermute | solution.py:265
  3.0 56.3 %collective-permute-start.2 = (f32[1,5,16,256]{3,2,1,0:T(8,128)S(1)}, f32[1,5,16,256]{3,2,1,0:T(8,128)S(1)}, u32[]{:S(2)}, u32[]{:S(2)}) collective-permute-start(f32[1,5,16,256]{3,2,1,0:T(8,128)S(1)} %get-tuple-element.28), channel_id=1, source_target_pairs={{0,8},{8,16},{16,24},{24,32},{32,40},{40,48},{48,56},{56,64},{64,7... | collective-permute-start | bytes 245768 | tf_op jit(solution)/shard_map/ppermute | solution.py:265
  10.0 16.8 %copy-start.1 = (f32[4,16,3,256]{3,1,2,0:T(8,128)S(1)}, f32[4,16,3,256]{3,1,2,0:T(8,128)}, u32[]{:S(2)}) copy-start(f32[4,16,3,256]{3,1,2,0:T(8,128)} %param.7) | copy-start | bytes 589828
  10.0 16.8 %copy-start.2 = (f32[4,16,256]{2,1,0:T(8,128)S(1)}, f32[4,16,256]{2,1,0:T(8,128)}, u32[]{:S(2)}) copy-start(f32[4,16,256]{2,1,0:T(8,128)} %param.9) | copy-start | bytes 196612
  10.1 16.8 %copy-start.3 = (f32[4,16,256]{2,1,0:T(8,128)S(1)}, f32[4,16,256]{2,1,0:T(8,128)}, u32[]{:S(2)}) copy-start(f32[4,16,256]{2,1,0:T(8,128)} %param.8) | copy-start | bytes 196612
  10.1 33.5 %all-to-all-start = ((f32[64,3,4,128]{3,2,1,0:T(4,128)}), f32[64,3,4,128]{3,2,1,0:T(4,128)S(1)}, u32[]{:S(2)}, u32[]{:S(2)}) async-start(f32[64,3,4,128]{3,2,1,0:T(4,128)} %bitcast.46), calls=%async_computation | async-start | bytes 786432 | tf_op jit(solution)/shard_map/all_to_all | solution.py:313
  26.9 32.4 %collective-permute-start.3 = (f32[4,5,1,256]{3,2,1,0:T(1,128)S(1)}, f32[4,5,1,256]{3,2,1,0:T(1,128)S(1)}, u32[]{:S(2)}, u32[]{:S(2)}) collective-permute-start(f32[4,5,1,256]{3,2,1,0:T(1,128)S(1)} %get-tuple-element.33), channel_id=1, source_target_pairs={{2,0},{4,2},{6,4},{3,1},{5,3},{7,5},{10,8},{12,10},{14,12},{11,9},... | collective-permute-start | bytes 61448 | tf_op jit(solution)/shard_map/ppermute | solution.py:265
  29.6 29.6 %collective-permute-start.4 = (f32[4,5,1,256]{3,2,1,0:T(1,128)S(1)}, f32[4,5,1,256]{3,2,1,0:T(1,128)S(1)}, u32[]{:S(2)}, u32[]{:S(2)}) collective-permute-start(f32[4,5,1,256]{3,2,1,0:T(1,128)S(1)} %get-tuple-element.32), channel_id=1, source_target_pairs={{0,2},{2,4},{4,6},{1,3},{3,5},{5,7},{8,10},{10,12},{12,14},{9,11},... | collective-permute-start | bytes 61448 | tf_op jit(solution)/shard_map/ppermute | solution.py:265
  43.5 0.8 copy-start
  57.3 3.6 %collective-permute-start = (bf16[512,256]{1,0:T(8,128)(2,1)}, bf16[512,256]{1,0:T(8,128)(2,1)S(1)}, u32[]{:S(2)}, u32[]{:S(2)}) collective-permute-start(bf16[512,256]{1,0:T(8,128)(2,1)} %spread.1.mine_ref), channel_id=1, source_target_pairs={{0,1},{1,0},{2,3},{3,2},{4,5},{5,4},{6,7},{7,6},{8,9},{9,8},{10,11... | collective-permute-start | bytes 786440 | tf_op jit(solution)/shard_map/ppermute | solution.py:333
  60.9 0.7 copy-start.4
  63.7 6.0 %collective-permute-start.5 = (bf16[216,256]{1,0:T(8,128)(2,1)}, bf16[216,256]{1,0:T(8,128)(2,1)S(1)}, u32[]{:S(2)}, u32[]{:S(2)}) collective-permute-start(bf16[216,256]{1,0:T(8,128)(2,1)} %get-tuple-element.14), channel_id=1, source_target_pairs={{0,8},{8,16},{16,24},{24,32},{32,40},{40,48},{48,56},{56,64},{64,7... | collective-permute-start | bytes 331784 | tf_op jit(solution)/shard_map/ppermute | solution.py:265
  66.8 6.9 %collective-permute-start.6 = (bf16[216,256]{1,0:T(8,128)(2,1)}, bf16[216,256]{1,0:T(8,128)(2,1)S(1)}, u32[]{:S(2)}, u32[]{:S(2)}) collective-permute-start(bf16[216,256]{1,0:T(8,128)(2,1)} %get-tuple-element.15), channel_id=1, source_target_pairs={{8,0},{16,8},{24,16},{32,24},{40,32},{48,40},{56,48},{64,56},{72,6... | collective-permute-start | bytes 331784 | tf_op jit(solution)/shard_map/ppermute | solution.py:265
  69.7 4.0 %copy-start.5 = (bf16[216,256]{1,0:T(8,128)(2,1)}, bf16[216,256]{1,0:T(8,128)(2,1)S(1)}, u32[]{:S(2)}) copy-start(bf16[216,256]{1,0:T(8,128)(2,1)S(1)} %collective-permute-done.5.left_ref) | copy-start | bytes 331780
  73.7 0.6 copy-start.6
  76.3 6.5 %collective-permute-start.7 = (bf16[24,768]{1,0:T(8,128)(2,1)}, bf16[24,768]{1,0:T(8,128)(2,1)S(1)}, u32[]{:S(2)}, u32[]{:S(2)}) collective-permute-start(bf16[24,768]{1,0:T(8,128)(2,1)} %get-tuple-element.17), channel_id=1, source_target_pairs={{0,2},{2,4},{4,6},{1,3},{3,5},{5,7},{8,10},{10,12},{12,14},{9,11},... | collective-permute-start | bytes 110600 | tf_op jit(solution)/shard_map/ppermute | solution.py:265
  77.6 6.5 %collective-permute-start.8 = (bf16[24,768]{1,0:T(8,128)(2,1)}, bf16[24,768]{1,0:T(8,128)(2,1)S(1)}, u32[]{:S(2)}, u32[]{:S(2)}) collective-permute-start(bf16[24,768]{1,0:T(8,128)(2,1)} %get-tuple-element.18), channel_id=1, source_target_pairs={{2,0},{4,2},{6,4},{3,1},{5,3},{7,5},{10,8},{12,10},{14,12},{11,9},... | collective-permute-start | bytes 110600 | tf_op jit(solution)/shard_map/ppermute | solution.py:265
  82.8 1.3 %copy-start.7 = (bf16[24,768]{1,0:T(8,128)(2,1)}, bf16[24,768]{1,0:T(8,128)(2,1)S(1)}, u32[]{:S(2)}) copy-start(bf16[24,768]{1,0:T(8,128)(2,1)S(1)} %collective-permute-done.7.refs_3_) | copy-start | bytes 110596
  84.1 0.6 copy-start.8

commit v2 on v1

v2 whole, which is shorter than its diff:
```python
import math

import jax
import jax.numpy as jnp
from jax import lax
from jax.experimental import pallas as pl
from jax.experimental.pallas import tpu as pltpu
from jax.sharding import PartitionSpec as P

M = 128
NZ = 256
YP = 24
XE = 7
ROWS = XE * YP
ROWS_PAD = 176
FIELD = 512
GROUP = 32
PAIR = 2
TURNS = 16

VMEM = pl.BlockSpec(memory_space=pltpu.VMEM)
SMEM = pl.BlockSpec(memory_space=pltpu.SMEM)


def iota(shape, dim):
    return lax.broadcasted_iota(jnp.int32, shape, dim)


def pack_kernel(blocks, slab_ref, offset_ref, base_ref, force_ref, out_ref, pos_ref, count, coords):
    slots = out_ref.shape[0] // 6
    out_ref[...] = jnp.zeros_like(out_ref)
    coords[...] = base_ref[...].astype(jnp.float32) + offset_ref[...]

    def clear(i, carry):
        count[i] = 0
        return carry

    lax.fori_loop(0, slots // 2, clear, 0)
    for b in range(blocks):
        slab = slab_ref[b]
        place = count[slab]
        count[slab] = place + 1
        slot = slab * 2 + place
        pos_ref[b] = slot
        for j in range(3):
            out_ref[pl.ds(slot * 6 + j, 1), :] = coords[j, b : b + 1, :]
            out_ref[pl.ds(slot * 6 + 3 + j, 1), :] = force_ref[j, b : b + 1, :]


def prepare_weights(load_ref, base_ref, weight_ref):
    rows = load_ref.shape[0]
    step = math.gcd(rows, 64)

    def turn(i, carry):
        at = pl.ds(pl.multiple_of(i * step, step), step)
        place = load_ref[at, :]
        base = jnp.floor(place)
        part = place - base
        root = jnp.sqrt(1.0 + 4.0 * part * (1.0 - part)) * 0.125
        falling = (3.0 - 2.0 * part) * 0.125
        rising = (1.0 + 2.0 * part) * 0.125
        base_ref[at, :] = base.astype(jnp.int32)
        weight_ref[0, at, :] = falling - root
        weight_ref[1, at, :] = falling + root
        weight_ref[2, at, :] = rising + root
        weight_ref[3, at, :] = rising - root
        return carry

    lax.fori_loop(0, rows // step, turn, 0)


def pick(index, weights):
    out = jnp.where(index == 0, weights[0], 0.0)
    for j in range(1, 4):
        out = jnp.where(index == j, weights[j], out)
    return out


def row8(ref, row):
    return jnp.broadcast_to(ref[pl.ds(row, 1), :], (8, M))


def block_weights(base_ref, weight_ref, row, row_x):
    sub = iota((8, M), 0)
    bx = row8(base_ref, row)
    by = row8(base_ref, row + 1)
    bz = row8(base_ref, row + 2)
    wx_in = [row8(weight_ref.at[j], row) for j in range(4)]
    wy_in = [row8(weight_ref.at[j], row + 1) for j in range(4)]
    wz_in = [row8(weight_ref.at[j], row + 2) for j in range(4)]
    row_x[...] = pick(sub - bx, wx_in)
    along_x = [jnp.broadcast_to(row_x[x : x + 1, :], (8, M)) for x in range(XE)]
    cells_y = [
        sub + 1,
        sub + 9,
        jnp.where(sub < 2, sub + 17, jnp.where(sub == 7, 0, -100)),
    ]
    along_y = [pick(cell - by, wy_in) for cell in cells_y]
    tiles = []
    values = []
    for half in range(2):
        lead = sub - bz + (1 + 8 * half)
        tiles.append(((15 - lead) >> 4).astype(jnp.float32))
        values.append(pick(lead & 15, wz_in))
    tile = jnp.concatenate(tiles, axis=0).astype(jnp.bfloat16)
    return along_x, along_y, tile, values


def expand(tile, value):
    zero = jnp.zeros((16, M), jnp.bfloat16)
    value = jnp.concatenate(value, axis=0).astype(jnp.bfloat16)
    return [jnp.where(tile == r, value, zero) for r in range(NZ // 16)]


def spread_kernel(load_ref, out_ref, base_ref, weight_ref, row_x, total):
    blocks = load_ref.shape[0] // 6
    prepare_weights(load_ref, base_ref, weight_ref)
    total[...] = jnp.zeros_like(total)

    def turn(i, carry):
        planes = []
        loads = []
        for g in range(GROUP):
            row = (i * GROUP + g) * 6
            along_x, along_y, tile, value = block_weights(
                base_ref, weight_ref, row, row_x.at[g]
            )
            loaded = []
            for c in range(3):
                force = row8(load_ref, row + 3 + c)
                loaded += expand(tile, [part * force for part in value])
            loads.append(jnp.concatenate(loaded, axis=0))
            plane = [along_x[x] * along_y[k] for x in range(XE) for k in range(3)]
            plane.append(jnp.zeros((8, M), jnp.float32))
            planes.append(jnp.concatenate(plane, axis=0).astype(jnp.bfloat16))
        total[...] += lax.dot_general(
            jnp.concatenate(loads, axis=1),
            jnp.concatenate(planes, axis=1),
            (((1,), (1,)), ((), ())),
            preferred_element_type=jnp.float32,
        )
        return carry

    lax.fori_loop(0, blocks // GROUP, turn, 0)
    out_ref[...] = jnp.transpose(total[...]).astype(out_ref.dtype)


def join_kernel(mine_ref, other_ref, old_ref, sum_ref, low_ref, high_ref):
    rim = 3 * YP
    sum_ref[...] = 0.5 * (
        mine_ref[0:ROWS, :].astype(jnp.float32) + other_ref[0:ROWS, :].astype(jnp.float32)
    )
    for x in range(4):
        for c in range(3):
            at = (x + 1) * YP
            sum_ref[at : at + 16, c * NZ : (c + 1) * NZ] += old_ref[x, c]
    low_ref[...] = sum_ref[0:rim, :].astype(jnp.bfloat16)
    high_ref[...] = sum_ref[ROWS - rim : ROWS, :].astype(jnp.bfloat16)


HIGH_ROWS = (15, 16, 17)
LOW_ROWS = (23, 0, 1)


def fold_kernel(sum_ref, left_ref, right_ref, out_ref, low_ref, high_ref, low, high):
    rim = 3 * YP
    out_ref[rim : ROWS - rim, :] = sum_ref[rim : ROWS - rim, :]
    out_ref[0:rim, :] = sum_ref[0:rim, :] + left_ref[...].astype(jnp.float32)
    out_ref[ROWS - rim : ROWS, :] = sum_ref[ROWS - rim : ROWS, :] + right_ref[...].astype(jnp.float32)
    low[...] = jnp.zeros_like(low)
    high[...] = jnp.zeros_like(high)
    for x in range(XE):
        for j in range(3):
            to = x * 3 + j
            at = x * YP + LOW_ROWS[j]
            low[to : to + 1, :] = out_ref[at : at + 1, :]
            at = x * YP + HIGH_ROWS[j]
            high[to : to + 1, :] = out_ref[at : at + 1, :]
    low_ref[...] = low[...].astype(jnp.bfloat16)
    high_ref[...] = high[...].astype(jnp.bfloat16)


def sample_kernel(
    fluid_count,
    sub_count,
    place_ref,
    load_ref,
    sum_ref,
    below_ref,
    above_ref,
    fresh_ref,
    out_ref,
    base_ref,
    weight_ref,
    row_x,
    grid,
    field,
    below,
    above,
):
    blocks = load_ref.shape[0] // 6
    prepare_weights(load_ref, base_ref, weight_ref)
    grid[...] = sum_ref[...]
    below[...] = below_ref[...].astype(jnp.float32)
    above[...] = above_ref[...].astype(jnp.float32)
    for x in range(XE):
        for j in range(3):
            come = x * 3 + j
            at = x * YP + LOW_ROWS[j]
            grid[at : at + 1, :] += below[come : come + 1, :]
            at = x * YP + HIGH_ROWS[j]
            grid[at : at + 1, :] += above[come : come + 1, :]
    for x in range(4):
        for c in range(3):
            at = (x + 1) * YP
            fresh_ref[x, c] = grid[at : at + 16, c * NZ : (c + 1) * NZ]
    first = place_ref[0]
    second = place_ref[1]
    sub = iota((8, 3 * NZ), 0)
    inside = ((sub < 2) & (second < sub_count - 1)) | ((sub == 7) & (second > 0))
    for x in range(XE):
        at = x * YP + 16
        grid[at : at + 8, :] = jnp.where(inside, grid[at : at + 8, :], 0.0)

    @pl.when(first == 0)
    def _():
        grid[0:YP, :] = jnp.zeros((YP, 3 * NZ), jnp.float32)

    @pl.when(first == fluid_count - 1)
    def _():
        grid[5 * YP : ROWS, :] = jnp.zeros((2 * YP, 3 * NZ), jnp.float32)

    rows = [grid[:, c * NZ : (c + 1) * NZ] for c in range(3)]
    rows.append(jnp.zeros((FIELD - 3 * ROWS, NZ), jnp.float32))
    field[...] = jnp.concatenate(rows, axis=0).astype(jnp.bfloat16)

    def turn(i, carry):
        for t in range(TURNS):
            block = (i * TURNS + t) * PAIR
            parts = []
            depth = []
            for g in range(PAIR):
                along_x, along_y, tile, value = block_weights(
                    base_ref, weight_ref, (block + g) * 6, row_x.at[t * PAIR + g]
                )
                parts.append((along_x, along_y))
                depth.append(jnp.concatenate(expand(tile, value), axis=0))
            seen = lax.dot_general(
                field[...],
                jnp.concatenate(depth, axis=1),
                (((1,), (0,)), ((), ())),
                preferred_element_type=jnp.float32,
            )
            for g in range(PAIR):
                along_x, along_y = parts[g]
                for c in range(3):
                    total = 0.0
                    for k in range(3):
                        inner = 0.0
                        for x in range(XE):
                            at = c * ROWS + x * YP + k * 8
                            inner = inner + along_x[x] * seen[at : at + 8, g * M : (g + 1) * M]
                        total = total + inner * along_y[k]
                    out_ref[pl.ds((block + g) * 3 + c, 1), :] = jnp.sum(
                        total, axis=0, keepdims=True
                    )
        return carry

    lax.fori_loop(0, blocks // (PAIR * TURNS), turn, 0)


def take_kernel(blocks, pos_ref, in_ref, out_ref):
    for b in range(blocks):
        slot = pos_ref[b]
        for c in range(3):
            out_ref[c, b : b + 1, :] = in_ref[pl.ds(slot * 3 + c, 1), :]


def shift(array, axis, by):
    count = lax.axis_size(axis)
    if by > 0:
        pairs = [(i, i + 1) for i in range(count - 1)]
    else:
        pairs = [(i + 1, i) for i in range(count - 1)]
    return lax.ppermute(array, axis, pairs)


def old_part(velocity, pressure, viscosity):
    v = jnp.transpose(velocity, (0, 2, 1, 3))
    p = pressure[:, None]
    n = viscosity[:, None]
    every = jnp.concatenate([v, p, n], axis=1)
    before_x = shift(every[-1:], "fluid", 1)
    after_x = shift(every[:1], "fluid", -1)
    before_y = shift(every[:, :, -1:], "sub", 1)
    after_y = shift(every[:, :, :1], "sub", -1)
    zero = jnp.zeros_like(every[..., :1])
    around = (
        jnp.concatenate([every[1:], after_x], axis=0),
        jnp.concatenate([before_x, every[:-1]], axis=0),
        jnp.concatenate([every[:, :, 1:], after_y], axis=2),
        jnp.concatenate([before_y, every[:, :, :-1]], axis=2),
        jnp.concatenate([every[..., 1:], zero], axis=3),
        jnp.concatenate([zero, every[..., :-1]], axis=3),
    )
    viscous = jnp.zeros_like(v)
    for near in around:
        viscous = viscous + 0.5 * (n + near[:, 4:5]) * (near[:, 0:3] - v)
    gradient = jnp.concatenate([around[k][:, 3:4] - p for k in (0, 2, 4)], axis=1)
    return v + 0.5 * (viscous - gradient)


def grant(mib):
    return pltpu.CompilerParams(vmem_limit_bytes=mib * 1024 * 1024)


def spread(arrived):
    return pl.pallas_call(
        spread_kernel,
        out_shape=jax.ShapeDtypeStruct((ROWS_PAD, 3 * NZ), jnp.bfloat16),
        in_specs=[VMEM],
        out_specs=VMEM,
        scratch_shapes=[
            pltpu.VMEM(arrived.shape, jnp.int32),
            pltpu.VMEM((4, *arrived.shape), jnp.float32),
            pltpu.VMEM((GROUP, 8, M), jnp.float32),
            pltpu.VMEM((3 * NZ, ROWS_PAD), jnp.float32),
        ],
        compiler_params=grant(16),
        name="spread",
    )(arrived)


def sample(slabs, subs, place, arrived, folded, from_below, from_above):
    lanes = 3 * NZ
    return pl.pallas_call(
        lambda *refs: sample_kernel(slabs, subs, *refs),
        out_shape=(
            jax.ShapeDtypeStruct((4, 3, 16, NZ), jnp.float32),
            jax.ShapeDtypeStruct((arrived.shape[0] // 2, M), jnp.float32),
        ),
        in_specs=[SMEM] + [VMEM] * 4,
        out_specs=(VMEM, VMEM),
        scratch_shapes=[
            pltpu.VMEM(arrived.shape, jnp.int32),
            pltpu.VMEM((4, *arrived.shape), jnp.float32),
            pltpu.VMEM((PAIR * TURNS, 8, M), jnp.float32),
            pltpu.VMEM((ROWS, lanes), jnp.float32),
            pltpu.VMEM((FIELD, NZ), jnp.bfloat16),
            pltpu.VMEM((24, lanes), jnp.float32),
            pltpu.VMEM((24, lanes), jnp.float32),
        ],
        compiler_params=grant(16),
        name="sample",
    )(place, arrived, folded, from_below, from_above)


def body(velocity, pressure, viscosity, marker_force, marker_offset, cell_base, block_slab):
    f32, bf16 = jnp.float32, jnp.bfloat16
    shape = jax.ShapeDtypeStruct
    blocks = marker_force.shape[0]
    slabs = lax.axis_size("fluid")
    subs = lax.axis_size("sub")
    slots = 2 * slabs
    lanes = 3 * NZ
    swap01 = lambda array: jnp.transpose(array, (1, 0, 2))
    payload, position = pl.pallas_call(
        lambda *refs: pack_kernel(blocks, *refs),
        out_shape=(shape((slots * 6, M), f32), shape((blocks,), jnp.int32)),
        in_specs=[SMEM, VMEM, VMEM, VMEM],
        out_specs=(VMEM, SMEM),
        scratch_shapes=[pltpu.SMEM((slabs,), jnp.int32), pltpu.VMEM((3, blocks, M), f32)],
        compiler_params=grant(60),
        name="pack",
    )(block_slab[:, 0], swap01(marker_offset), swap01(cell_base), swap01(marker_force))
    payload, velocity, pressure, viscosity = lax.optimization_barrier(
        (payload, velocity, pressure, viscosity)
    )
    arrived = lax.all_to_all(
        payload.reshape(slabs, 3, 4, M), "fluid", split_axis=0, concat_axis=0, tiled=True
    ).reshape(slots * 6, M)
    old = old_part(velocity, pressure, viscosity)
    partial_grid = spread(arrived)
    other_grid = lax.ppermute(partial_grid, "struct", [(0, 1), (1, 0)])
    rim = 3 * YP
    summed, low, high = pl.pallas_call(
        join_kernel,
        out_shape=(shape((ROWS, lanes), f32), shape((rim, lanes), bf16), shape((rim, lanes), bf16)),
        in_specs=[VMEM] * 3,
        out_specs=(VMEM,) * 3,
        compiler_params=grant(6),
        name="join",
    )(partial_grid, other_grid, old)
    from_left = shift(high, "fluid", 1)
    from_right = shift(low, "fluid", -1)
    folded, low, high = pl.pallas_call(
        fold_kernel,
        out_shape=(shape((ROWS, lanes), f32), shape((24, lanes), bf16), shape((24, lanes), bf16)),
        in_specs=[VMEM] * 3,
        out_specs=(VMEM,) * 3,
        scratch_shapes=[pltpu.VMEM((24, lanes), f32)] * 2,
        compiler_params=grant(6),
        name="fold",
    )(summed, from_left, from_right)
    from_below = shift(high, "sub", 1)
    from_above = shift(low, "sub", -1)
    place = jnp.stack([lax.axis_index("fluid"), lax.axis_index("sub")]).astype(jnp.int32)
    fresh, sampled = sample(slabs, subs, place, arrived, folded, from_below, from_above)
    returned = lax.all_to_all(
        sampled.reshape(slabs, 3, 2, M), "fluid", split_axis=0, concat_axis=0, tiled=True
    ).reshape(slots * 3, M)
    result = pl.pallas_call(
        lambda *refs: take_kernel(blocks, *refs),
        out_shape=shape((3, blocks, M), f32),
        in_specs=[SMEM, VMEM],
        out_specs=VMEM,
        compiler_params=grant(2),
        name="take",
    )(position, returned)
    return (jnp.transpose(fresh, (0, 2, 1, 3)), swap01(result))


def solution(mesh):
    return jax.shard_map(
        body,
        mesh=mesh,
        in_specs=(
            P("fluid", "sub", None, None),
            P("fluid", "sub", None),
            P("fluid", "sub", None),
            P(("fluid", "sub", "struct"), None, None),
            P(("fluid", "sub", "struct"), None, None),
            P(("fluid", "sub", "struct"), None, None),
            P(("fluid", "sub", "struct"), None),
        ),
        out_specs=(P("fluid", "sub", None, None), P(("fluid", "sub", "struct"), None, None)),
        check_vma=False,
    )
```

time: 130 us -> 105 us (0.81)
  the two profiles are of different devices: /device:TPU:6 before, /device:TPU:2 now
where the time goes in v2:
time: 105 us; the launch traced here: 104 us
  starting transfers between devices  40.6 us (39%)
  blocking collectives  22 us (21%)
  waiting for transfers between devices  20.4 us (19%)
  Pallas kernels  18.3 us (17%)
  other arithmetic  1.33 us (1%)
    all_to_all x1, blocking collectives, body(): lax.all_to_all(sampled.reshape(slabs, 3, 2, M), 'fluid', split_axis=0, co...  22 us
    ppermute x8, starting transfers between devices, shift(): return lax.ppermute(array, axis, pairs)  21.9 us
    all_to_all x1, starting transfers between devices, body(): lax.all_to_all(payload.reshape(slabs, 3, 4, M), 'fluid', split_axis=0, co...  16.7 us
    all_to_all x1, waiting for transfers between devices, body(): lax.all_to_all(payload.reshape(slabs, 3, 4, M), 'fluid', split_axis=0, co...  10.5 us
    ppermute x8, waiting for transfers between devices, shift(): return lax.ppermute(array, axis, pairs)  8.73 us
    pallas_call x1, Pallas kernels, spread(): pl.pallas_call(spread_kernel, out_shape=jax.ShapeDtypeStruct((ROWS_PAD, 3...  7.96 us
    pallas_call x1, Pallas kernels, sample(): pl.pallas_call(lambda *refs: sample_kernel(slabs, subs, *refs), out_shape...  6.27 us
    pallas_call x1, Pallas kernels, body(): pl.pallas_call(lambda *refs: pack_kernel(blocks, *refs), out_shape=(shape...  2.51 us
  transfers between devices with their start and end apart: 10, of which 5 were waited for; matrix products, arithmetic and copies ran while one was open for 1% of the time, Pallas kernels for 8%

profile of v2, /device:TPU:2, one launch (start us, length us, event | category | flops | bytes accessed | tf_op | source)
XLA Modules:
  0.0 104.3 jit_solution(8503459967732782099)
XLA Ops:
  0.7 2.5 %pack.1 = (f32[768,128]{1,0:T(8,128)}, s32[64]{0:T(128)}) custom-call(s32[64]{0:T(128)} %bitcast.51, f32[3,64,128]{2,1,0:T(8,128)} %bitcast.47, s32[3,64,128]{2,1,0:T(8,128)} %bitcast.48, f32[3,64,128]{2,1,0:T(8,128)} %bitcast.49), custom_call_target="tpu_custom_call" | custom-call | tf_op jit(solution)/shard_map/pack/pallas_call | solution.py:367
  3.2 0.9 pad_maximum_fusion
  4.1 1.3 %collective-permute-start.1 = (f32[1,5,16,256]{3,2,1,0:T(8,128)S(1)}, f32[1,5,16,256]{3,2,1,0:T(8,128)S(1)}, u32[]{:S(2)}, u32[]{:S(2)}) collective-permute-start(f32[1,5,16,256]{3,2,1,0:T(8,128)S(1)} %get-tuple-element.37), channel_id=1, source_target_pairs={{8,0},{16,8},{24,16},{32,24},{40,32},{48,40},{56,48},{64,56},{72,6... | collective-permute-start | bytes 245768 | tf_op jit(solution)/shard_map/ppermute | solution.py:285
  5.4 4.6 %collective-permute-start.2 = (f32[1,5,16,256]{3,2,1,0:T(8,128)S(1)}, f32[1,5,16,256]{3,2,1,0:T(8,128)S(1)}, u32[]{:S(2)}, u32[]{:S(2)}) collective-permute-start(f32[1,5,16,256]{3,2,1,0:T(8,128)S(1)} %get-tuple-element.36), channel_id=1, source_target_pairs={{0,8},{8,16},{16,24},{24,32},{32,40},{40,48},{48,56},{56,64},{64,7... | collective-permute-start | bytes 245768 | tf_op jit(solution)/shard_map/ppermute | solution.py:285
  10.0 16.7 %all-to-all-start = ((f32[64,3,4,128]{3,2,1,0:T(4,128)}), f32[64,3,4,128]{3,2,1,0:T(4,128)S(1)}, u32[]{:S(2)}, u32[]{:S(2)}) async-start(f32[64,3,4,128]{3,2,1,0:T(4,128)} %bitcast.6), calls=%async_computation | async-start | bytes 786432 | tf_op jit(solution)/shard_map/all_to_all | solution.py:379
  26.7 2.4 %collective-permute-start.3 = (f32[4,5,1,256]{3,2,1,0:T(1,128)S(1)}, f32[4,5,1,256]{3,2,1,0:T(1,128)S(1)}, u32[]{:S(2)}, u32[]{:S(2)}) collective-permute-start(f32[4,5,1,256]{3,2,1,0:T(1,128)S(1)} %get-tuple-element.41), channel_id=1, source_target_pairs={{2,0},{4,2},{6,4},{3,1},{5,3},{7,5},{10,8},{12,10},{14,12},{11,9},... | collective-permute-start | bytes 61448 | tf_op jit(solution)/shard_map/ppermute | solution.py:285
  29.2 3.4 %collective-permute-start.4 = (f32[4,5,1,256]{3,2,1,0:T(1,128)S(1)}, f32[4,5,1,256]{3,2,1,0:T(1,128)S(1)}, u32[]{:S(2)}, u32[]{:S(2)}) collective-permute-start(f32[4,5,1,256]{3,2,1,0:T(1,128)S(1)} %get-tuple-element.40), channel_id=1, source_target_pairs={{0,2},{2,4},{4,6},{1,3},{3,5},{5,7},{8,10},{10,12},{12,14},{9,11},... | collective-permute-start | bytes 61448 | tf_op jit(solution)/shard_map/ppermute | solution.py:285
  32.7 0.2 fusion.42
  32.9 10.5 %all-to-all-done = f32[64,3,4,128]{3,2,1,0:T(4,128)S(1)} async-done(((f32[64,3,4,128]{3,2,1,0:T(4,128)}), f32[64,3,4,128]{3,2,1,0:T(4,128)S(1)}, u32[]{:S(2)}, u32[]{:S(2)}) %all-to-all-start) | async-done | bytes 393248 | tf_op jit(solution)/shard_map/all_to_all | solution.py:379
  43.4 8.0 %spread.1.mine_ref = bf16[176,768]{1,0:T(8,128)(2,1)S(1)} custom-call(f32[768,128]{1,0:T(8,128)S(1)} %bitcast.37), custom_call_target="tpu_custom_call" | custom-call | tf_op jit(solution)/shard_map/spread/pallas_call | solution.py:318
  51.4 1.9 %collective-permute-start = (bf16[176,768]{1,0:T(8,128)(2,1)S(1)}, bf16[176,768]{1,0:T(8,128)(2,1)S(1)}, u32[]{:S(2)}, u32[]{:S(2)}) collective-permute-start(bf16[176,768]{1,0:T(8,128)(2,1)S(1)} %spread.1.mine_ref), channel_id=1, source_target_pairs={{0,1},{1,0},{2,3},{3,2},{4,5},{5,4},{6,7},{7,6},{8,9},{9,8},{10,11... | collective-permute-start | bytes 811016 | tf_op jit(solution)/shard_map/ppermute | solution.py:384
  53.5 0.3 fusion.6.old_ref
  53.7 1.1 %collective-permute-done.other_ref = bf16[176,768]{1,0:T(8,128)(2,1)S(1)} collective-permute-done((bf16[176,768]{1,0:T(8,128)(2,1)S(1)}, bf16[176,768]{1,0:T(8,128)(2,1)S(1)}, u32[]{:S(2)}, u32[]{:S(2)}) %collective-permute-start) | collective-permute-done | bytes 270368 | tf_op jit(solution)/shard_map/ppermute | solution.py:384
  55.0 3.1 %collective-permute-start.5 = (bf16[72,768]{1,0:T(8,128)(2,1)S(1)}, bf16[72,768]{1,0:T(8,128)(2,1)S(1)}, u32[]{:S(2)}, u32[]{:S(2)}) collective-permute-start(bf16[72,768]{1,0:T(8,128)(2,1)S(1)} %get-tuple-element.22), channel_id=1, source_target_pairs={{0,8},{8,16},{16,24},{24,32},{32,40},{40,48},{48,56},{56,64},{64,7... | collective-permute-start | bytes 331784 | tf_op jit(solution)/shard_map/ppermute | solution.py:285
  58.1 1.3 %collective-permute-start.6 = (bf16[72,768]{1,0:T(8,128)(2,1)S(1)}, bf16[72,768]{1,0:T(8,128)(2,1)S(1)}, u32[]{:S(2)}, u32[]{:S(2)}) collective-permute-start(bf16[72,768]{1,0:T(8,128)(2,1)S(1)} %get-tuple-element.23), channel_id=1, source_target_pairs={{8,0},{16,8},{24,16},{32,24},{40,32},{48,40},{56,48},{64,56},{72,6... | collective-permute-start | bytes 331784 | tf_op jit(solution)/shard_map/ppermute | solution.py:285
  59.4 1.3 %collective-permute-done.5.left_ref = bf16[72,768]{1,0:T(8,128)(2,1)S(1)} collective-permute-done((bf16[72,768]{1,0:T(8,128)(2,1)S(1)}, bf16[72,768]{1,0:T(8,128)(2,1)S(1)}, u32[]{:S(2)}, u32[]{:S(2)}) %collective-permute-start.5) | collective-permute-done | bytes 110624 | tf_op jit(solution)/shard_map/ppermute | solution.py:285
  60.7 4.1 %collective-permute-done.6.right_ref = bf16[72,768]{1,0:T(8,128)(2,1)S(1)} collective-permute-done((bf16[72,768]{1,0:T(8,128)(2,1)S(1)}, bf16[72,768]{1,0:T(8,128)(2,1)S(1)}, u32[]{:S(2)}, u32[]{:S(2)}) %collective-permute-start.6) | collective-permute-done | bytes 110624 | tf_op jit(solution)/shard_map/ppermute | solution.py:285
  64.9 3.4 %collective-permute-start.7 = (bf16[24,768]{1,0:T(8,128)(2,1)S(1)}, bf16[24,768]{1,0:T(8,128)(2,1)S(1)}, u32[]{:S(2)}, u32[]{:S(2)}) collective-permute-start(bf16[24,768]{1,0:T(8,128)(2,1)S(1)} %get-tuple-element.25), channel_id=1, source_target_pairs={{0,2},{2,4},{4,6},{1,3},{3,5},{5,7},{8,10},{10,12},{12,14},{9,11},... | collective-permute-start | bytes 110600 | tf_op jit(solution)/shard_map/ppermute | solution.py:285
  68.3 2.5 %collective-permute-start.8 = (bf16[24,768]{1,0:T(8,128)(2,1)S(1)}, bf16[24,768]{1,0:T(8,128)(2,1)S(1)}, u32[]{:S(2)}, u32[]{:S(2)}) collective-permute-start(bf16[24,768]{1,0:T(8,128)(2,1)S(1)} %get-tuple-element.26), channel_id=1, source_target_pairs={{2,0},{4,2},{6,4},{3,1},{5,3},{7,5},{10,8},{12,10},{14,12},{11,9},... | collective-permute-start | bytes 110600 | tf_op jit(solution)/shard_map/ppermute | solution.py:285
  70.8 3.3 %collective-permute-done.8.refs_4_ = bf16[24,768]{1,0:T(8,128)(2,1)S(1)} collective-permute-done((bf16[24,768]{1,0:T(8,128)(2,1)S(1)}, bf16[24,768]{1,0:T(8,128)(2,1)S(1)}, u32[]{:S(2)}, u32[]{:S(2)}) %collective-permute-start.8) | collective-permute-done | bytes 36896 | tf_op jit(solution)/shard_map/ppermute | solution.py:285
  74.1 6.3 %sample.1 = (f32[4,3,16,256]{3,2,1,0:T(8,128)}, f32[384,128]{1,0:T(8,128)S(1)}) custom-call(s32[2]{0:T(128)S(1)} %pad_add_fusion.refs_0_, f32[768,128]{1,0:T(8,128)S(1)} %bitcast.38, f32[168,768]{1,0:T(8,128)S(1)} %get-tuple-element.24.refs_2_, bf16[24,768]{1,0:T(8,128)(2,1)S(1)} %collective-permute-done.7.refs_3_, ...), custom_call_target="tpu_custom_call" | custom-call | tf_op jit(solution)/shard_map/sample/pallas_call | solution.py:336
  80.4 22.0 %all_to_all.10 = f32[64,3,2,128]{3,2,1,0:T(2,128)S(1)} all-to-all(f32[64,3,2,128]{3,2,1,0:T(2,128)S(1)} %bitcast.40), channel_id=1, replica_groups=mesh['fluid'=64,'sub'=4,'struct'=2] {'fluid'}, dimensions={0} | all-to-all | bytes 393216 | tf_op jit(solution)/shard_map/all_to_all | solution.py:409
  102.4 0.6 copy-done
  103.0 1.3 %take.1 = f32[3,64,128]{2,1,0:T(8,128)} custom-call(s32[64]{0:T(128)S(1)} %copy-done, f32[384,128]{1,0:T(8,128)S(1)} %bitcast.39), custom_call_target="tpu_custom_call" | custom-call | tf_op jit(solution)/shard_map/take/pallas_call | solution.py:412
  (20 shorter events, 0.6 us)
Async XLA Ops:
  0.6 2.5 %copy-start.1 = (f32[4,16,3,256]{3,1,2,0:T(8,128)S(1)}, f32[4,16,3,256]{3,1,2,0:T(8,128)}, u32[]{:S(2)}) copy-start(f32[4,16,3,256]{3,1,2,0:T(8,128)} %param.7) | copy-start | bytes 589828
  0.6 2.5 %copy-start.2 = (f32[4,16,256]{2,1,0:T(8,128)S(1)}, f32[4,16,256]{2,1,0:T(8,128)}, u32[]{:S(2)}) copy-start(f32[4,16,256]{2,1,0:T(8,128)} %param.9) | copy-start | bytes 196612
  4.1 49.3 %collective-permute-start.1 = (f32[1,5,16,256]{3,2,1,0:T(8,128)S(1)}, f32[1,5,16,256]{3,2,1,0:T(8,128)S(1)}, u32[]{:S(2)}, u32[]{:S(2)}) collective-permute-start(f32[1,5,16,256]{3,2,1,0:T(8,128)S(1)} %get-tuple-element.37), channel_id=1, source_target_pairs={{8,0},{16,8},{24,16},{32,24},{40,32},{48,40},{56,48},{64,56},{72,6... | collective-permute-start | bytes 245768 | tf_op jit(solution)/shard_map/ppermute | solution.py:285
  5.4 48.0 %collective-permute-start.2 = (f32[1,5,16,256]{3,2,1,0:T(8,128)S(1)}, f32[1,5,16,256]{3,2,1,0:T(8,128)S(1)}, u32[]{:S(2)}, u32[]{:S(2)}) collective-permute-start(f32[1,5,16,256]{3,2,1,0:T(8,128)S(1)} %get-tuple-element.36), channel_id=1, source_target_pairs={{0,8},{8,16},{16,24},{24,32},{32,40},{40,48},{48,56},{56,64},{64,7... | collective-permute-start | bytes 245768 | tf_op jit(solution)/shard_map/ppermute | solution.py:285
  9.9 16.8 %copy-start.3 = (f32[4,16,256]{2,1,0:T(8,128)S(1)}, f32[4,16,256]{2,1,0:T(8,128)}, u32[]{:S(2)}) copy-start(f32[4,16,256]{2,1,0:T(8,128)} %param.8) | copy-start | bytes 196612
  10.0 33.5 %all-to-all-start = ((f32[64,3,4,128]{3,2,1,0:T(4,128)}), f32[64,3,4,128]{3,2,1,0:T(4,128)S(1)}, u32[]{:S(2)}, u32[]{:S(2)}) async-start(f32[64,3,4,128]{3,2,1,0:T(4,128)} %bitcast.6), calls=%async_computation | async-start | bytes 786432 | tf_op jit(solution)/shard_map/all_to_all | solution.py:379
  26.7 26.6 %collective-permute-start.3 = (f32[4,5,1,256]{3,2,1,0:T(1,128)S(1)}, f32[4,5,1,256]{3,2,1,0:T(1,128)S(1)}, u32[]{:S(2)}, u32[]{:S(2)}) collective-permute-start(f32[4,5,1,256]{3,2,1,0:T(1,128)S(1)} %get-tuple-element.41), channel_id=1, source_target_pairs={{2,0},{4,2},{6,4},{3,1},{5,3},{7,5},{10,8},{12,10},{14,12},{11,9},... | collective-permute-start | bytes 61448 | tf_op jit(solution)/shard_map/ppermute | solution.py:285
  29.2 24.1 %collective-permute-start.4 = (f32[4,5,1,256]{3,2,1,0:T(1,128)S(1)}, f32[4,5,1,256]{3,2,1,0:T(1,128)S(1)}, u32[]{:S(2)}, u32[]{:S(2)}) collective-permute-start(f32[4,5,1,256]{3,2,1,0:T(1,128)S(1)} %get-tuple-element.40), channel_id=1, source_target_pairs={{0,2},{2,4},{4,6},{1,3},{3,5},{5,7},{8,10},{10,12},{12,14},{9,11},... | collective-permute-start | bytes 61448 | tf_op jit(solution)/shard_map/ppermute | solution.py:285
  51.4 3.4 %collective-permute-start = (bf16[176,768]{1,0:T(8,128)(2,1)S(1)}, bf16[176,768]{1,0:T(8,128)(2,1)S(1)}, u32[]{:S(2)}, u32[]{:S(2)}) collective-permute-start(bf16[176,768]{1,0:T(8,128)(2,1)S(1)} %spread.1.mine_ref), channel_id=1, source_target_pairs={{0,1},{1,0},{2,3},{3,2},{4,5},{5,4},{6,7},{7,6},{8,9},{9,8},{10,11... | collective-permute-start | bytes 811016 | tf_op jit(solution)/shard_map/ppermute | solution.py:384
  55.0 5.7 %collective-permute-start.5 = (bf16[72,768]{1,0:T(8,128)(2,1)S(1)}, bf16[72,768]{1,0:T(8,128)(2,1)S(1)}, u32[]{:S(2)}, u32[]{:S(2)}) collective-permute-start(bf16[72,768]{1,0:T(8,128)(2,1)S(1)} %get-tuple-element.22), channel_id=1, source_target_pairs={{0,8},{8,16},{16,24},{24,32},{32,40},{40,48},{48,56},{56,64},{64,7... | collective-permute-start | bytes 331784 | tf_op jit(solution)/shard_map/ppermute | solution.py:285
  58.1 6.7 %collective-permute-start.6 = (bf16[72,768]{1,0:T(8,128)(2,1)S(1)}, bf16[72,768]{1,0:T(8,128)(2,1)S(1)}, u32[]{:S(2)}, u32[]{:S(2)}) collective-permute-start(bf16[72,768]{1,0:T(8,128)(2,1)S(1)} %get-tuple-element.23), channel_id=1, source_target_pairs={{8,0},{16,8},{24,16},{32,24},{40,32},{48,40},{56,48},{64,56},{72,6... | collective-permute-start | bytes 331784 | tf_op jit(solution)/shard_map/ppermute | solution.py:285
  64.9 5.9 %collective-permute-start.7 = (bf16[24,768]{1,0:T(8,128)(2,1)S(1)}, bf16[24,768]{1,0:T(8,128)(2,1)S(1)}, u32[]{:S(2)}, u32[]{:S(2)}) collective-permute-start(bf16[24,768]{1,0:T(8,128)(2,1)S(1)} %get-tuple-element.25), channel_id=1, source_target_pairs={{0,2},{2,4},{4,6},{1,3},{3,5},{5,7},{8,10},{10,12},{12,14},{9,11},... | collective-permute-start | bytes 110600 | tf_op jit(solution)/shard_map/ppermute | solution.py:285
  68.3 5.9 %collective-permute-start.8 = (bf16[24,768]{1,0:T(8,128)(2,1)S(1)}, bf16[24,768]{1,0:T(8,128)(2,1)S(1)}, u32[]{:S(2)}, u32[]{:S(2)}) collective-permute-start(bf16[24,768]{1,0:T(8,128)(2,1)S(1)} %get-tuple-element.26), channel_id=1, source_target_pairs={{2,0},{4,2},{6,4},{3,1},{5,3},{7,5},{10,8},{12,10},{14,12},{11,9},... | collective-permute-start | bytes 110600 | tf_op jit(solution)/shard_map/ppermute | solution.py:285
  102.4 0.6 copy-start

commit v3 on v2

--- a/solution.py
+++ b/solution.py
@@ -31,11 +31,8 @@
     out_ref[...] = jnp.zeros_like(out_ref)
     coords[...] = base_ref[...].astype(jnp.float32) + offset_ref[...]
 
-    def clear(i, carry):
+    for i in range(slots // 2):
         count[i] = 0
-        return carry
-
-    lax.fori_loop(0, slots // 2, clear, 0)
     for b in range(blocks):
         slab = slab_ref[b]
         place = count[slab]
@@ -162,22 +159,31 @@
 LOW_ROWS = (23, 0, 1)
 
 
-def fold_kernel(sum_ref, left_ref, right_ref, out_ref, low_ref, high_ref, low, high):
+def fold_kernel(
+    sum_ref, left_ref, right_ref, edge_low_ref, edge_high_ref, out_ref, low_ref, high_ref, low, high
+):
     rim = 3 * YP
     out_ref[rim : ROWS - rim, :] = sum_ref[rim : ROWS - rim, :]
     out_ref[0:rim, :] = sum_ref[0:rim, :] + left_ref[...].astype(jnp.float32)
     out_ref[ROWS - rim : ROWS, :] = sum_ref[ROWS - rim : ROWS, :] + right_ref[...].astype(jnp.float32)
-    low[...] = jnp.zeros_like(low)
-    high[...] = jnp.zeros_like(high)
-    for x in range(XE):
-        for j in range(3):
-            to = x * 3 + j
-            at = x * YP + LOW_ROWS[j]
-            low[to : to + 1, :] = out_ref[at : at + 1, :]
-            at = x * YP + HIGH_ROWS[j]
-            high[to : to + 1, :] = out_ref[at : at + 1, :]
+    for sent, edge, rows in ((low, edge_low_ref, LOW_ROWS), (high, edge_high_ref, HIGH_ROWS)):
+        sent[...] = jnp.zeros_like(sent)
+        for x in range(XE):
+            for j in range(3):
+                at = x * YP + rows[j]
+                sent[x * 3 + j : x * 3 + j + 1, :] = out_ref[at : at + 1, :]
+        sent[24:32, :] = edge[:, 0 : 3 * NZ]
+        sent[32:40, 0 : 2 * NZ] = edge[:, 3 * NZ : 5 * NZ]
     low_ref[...] = low[...].astype(jnp.bfloat16)
     high_ref[...] = high[...].astype(jnp.bfloat16)
+
+
+def face_flux(before, after):
+    flux = []
+    thick = 0.25 * (before(4) + after(4))
+    for c in range(3):
+        flux.append(thick * (after(c) - before(c)))
+    return flux, 0.5 * (after(3) - before(3))
 
 
 def sample_kernel(
@@ -188,6 +194,8 @@
     sum_ref,
     below_ref,
     above_ref,
+    edge_low_ref,
+    edge_high_ref,
     fresh_ref,
     out_ref,
     base_ref,
@@ -203,13 +211,32 @@
     grid[...] = sum_ref[...]
     below[...] = below_ref[...].astype(jnp.float32)
     above[...] = above_ref[...].astype(jnp.float32)
-    for x in range(XE):
-        for j in range(3):
-            come = x * 3 + j
-            at = x * YP + LOW_ROWS[j]
-            grid[at : at + 1, :] += below[come : come + 1, :]
-            at = x * YP + HIGH_ROWS[j]
-            grid[at : at + 1, :] += above[come : come + 1, :]
+    mine_low = lambda f: edge_low_ref[:, f * NZ : (f + 1) * NZ]
+    mine_high = lambda f: edge_high_ref[:, f * NZ : (f + 1) * NZ]
+
+    def theirs(ref):
+        return lambda f: (
+            ref[24:32, f * NZ : (f + 1) * NZ]
+            if f < 3
+            else ref[32:40, (f - 3) * NZ : (f - 2) * NZ]
+        )
+
+    for come, rows, before, after in (
+        (below, LOW_ROWS, theirs(below), mine_low),
+        (above, HIGH_ROWS, mine_high, theirs(above)),
+    ):
+        flux, step = face_flux(before, after)
+        plus = jnp.concatenate([flux[0], flux[1] - step, flux[2]], axis=1)
+        minus = jnp.concatenate(flux, axis=1)
+        for x in range(XE):
+            for j in range(3):
+                more = come[x * 3 + j : x * 3 + j + 1, :]
+                if j == 0:
+                    more = more + plus[x : x + 1, :]
+                if j == 1:
+                    more = more - minus[x : x + 1, :]
+                at = x * YP + rows[j]
+                grid[at : at + 1, :] += more
     for x in range(4):
         for c in range(3):
             at = (x + 1) * YP
@@ -285,29 +312,53 @@
     return lax.ppermute(array, axis, pairs)
 
 
+def old_kernel(v_ref, p_ref, n_ref, before_ref, after_ref, out_ref, edge_low_ref, edge_high_ref):
+    rows, lanes = p_ref.shape[1:]
+    y = iota((rows, lanes), 0)
+    z = iota((rows, lanes), 1)
+    before = [before_ref[0, f].astype(jnp.float32) for f in range(5)]
+    after = [[after_ref[x, f].astype(jnp.float32) for f in range(5)] for x in range(2)]
+    every = [[v_ref[x, c] for c in range(3)] + [p_ref[x], n_ref[x]] for x in range(4)]
+    columns = [before, *every, *after]
+    for edge_ref, at in ((edge_low_ref, 0), (edge_high_ref, rows - 1)):
+        edge_ref[XE : XE + 1, :] = jnp.zeros((1, 5 * lanes), jnp.float32)
+        for x in range(XE):
+            for f in range(5):
+                edge_ref[x : x + 1, f * lanes : (f + 1) * lanes] = columns[x][f][at : at + 1, :]
+    steps = (
+        lambda x, f: columns[x + 1][f],
+        lambda x, f: columns[x - 1][f],
+        lambda x, f: jnp.where(y == rows - 1, columns[x][f], pltpu.roll(columns[x][f], rows - 1, 0)),
+        lambda x, f: jnp.where(y == 0, columns[x][f], pltpu.roll(columns[x][f], 1, 0)),
+        lambda x, f: jnp.where(z == lanes - 1, 0.0, pltpu.roll(columns[x][f], lanes - 1, 1)),
+        lambda x, f: jnp.where(z == 0, 0.0, pltpu.roll(columns[x][f], 1, 1)),
+    )
+    for x in range(1, 5):
+        thick = [0.25 * (columns[x][4] + step(x, 4)) for step in steps]
+        for c in range(3):
+            here = columns[x][c]
+            total = here - 0.5 * (steps[2 * c](x, 3) - columns[x][3])
+            for k in range(6):
+                total = total + thick[k] * (steps[k](x, c) - here)
+            out_ref[x - 1, c] = total
+
+
 def old_part(velocity, pressure, viscosity):
     v = jnp.transpose(velocity, (0, 2, 1, 3))
-    p = pressure[:, None]
-    n = viscosity[:, None]
-    every = jnp.concatenate([v, p, n], axis=1)
-    before_x = shift(every[-1:], "fluid", 1)
-    after_x = shift(every[:1], "fluid", -1)
-    before_y = shift(every[:, :, -1:], "sub", 1)
-    after_y = shift(every[:, :, :1], "sub", -1)
-    zero = jnp.zeros_like(every[..., :1])
-    around = (
-        jnp.concatenate([every[1:], after_x], axis=0),
-        jnp.concatenate([before_x, every[:-1]], axis=0),
-        jnp.concatenate([every[:, :, 1:], after_y], axis=2),
-        jnp.concatenate([before_y, every[:, :, :-1]], axis=2),
-        jnp.concatenate([every[..., 1:], zero], axis=3),
-        jnp.concatenate([zero, every[..., :-1]], axis=3),
-    )
-    viscous = jnp.zeros_like(v)
-    for near in around:
-        viscous = viscous + 0.5 * (n + near[:, 4:5]) * (near[:, 0:3] - v)
-    gradient = jnp.concatenate([around[k][:, 3:4] - p for k in (0, 2, 4)], axis=1)
-    return v + 0.5 * (viscous - gradient)
+    picked = lambda rows: jnp.concatenate(
+        [v[rows], pressure[rows][:, None], viscosity[rows][:, None]], axis=1
+    ).astype(jnp.bfloat16)
+    before = shift(picked(slice(3, 4)), "fluid", 1)
+    after = shift(picked(slice(0, 2)), "fluid", -1)
+    edge = jax.ShapeDtypeStruct((XE + 1, 5 * NZ), jnp.float32)
+    return pl.pallas_call(
+        old_kernel,
+        out_shape=(jax.ShapeDtypeStruct(v.shape, jnp.float32), edge, edge),
+        in_specs=[VMEM] * 5,
+        out_specs=(VMEM,) * 3,
+        compiler_params=grant(6),
+        name="old",
+    )(v, pressure, viscosity, before, after)
 
 
 def grant(mib):
@@ -331,7 +382,7 @@
     )(arrived)
 
 
-def sample(slabs, subs, place, arrived, folded, from_below, from_above):
+def sample(slabs, subs, place, arrived, folded, from_below, from_above, edge_low, edge_high):
     lanes = 3 * NZ
     return pl.pallas_call(
         lambda *refs: sample_kernel(slabs, subs, *refs),
@@ -339,7 +390,7 @@
             jax.ShapeDtypeStruct((4, 3, 16, NZ), jnp.float32),
             jax.ShapeDtypeStruct((arrived.shape[0] // 2, M), jnp.float32),
         ),
-        in_specs=[SMEM] + [VMEM] * 4,
+        in_specs=[SMEM] + [VMEM] * 6,
         out_specs=(VMEM, VMEM),
         scratch_shapes=[
             pltpu.VMEM(arrived.shape, jnp.int32),
@@ -347,12 +398,12 @@
             pltpu.VMEM((PAIR * TURNS, 8, M), jnp.float32),
             pltpu.VMEM((ROWS, lanes), jnp.float32),
             pltpu.VMEM((FIELD, NZ), jnp.bfloat16),
-            pltpu.VMEM((24, lanes), jnp.float32),
-            pltpu.VMEM((24, lanes), jnp.float32),
+            pltpu.VMEM((40, lanes), jnp.float32),
+            pltpu.VMEM((40, lanes), jnp.float32),
         ],
         compiler_params=grant(16),
         name="sample",
-    )(place, arrived, folded, from_below, from_above)
+    )(place, arrived, folded, from_below, from_above, edge_low, edge_high)
 
 
 def body(velocity, pressure, viscosity, marker_force, marker_offset, cell_base, block_slab):
@@ -379,7 +430,7 @@
     arrived = lax.all_to_all(
         payload.reshape(slabs, 3, 4, M), "fluid", split_axis=0, concat_axis=0, tiled=True
     ).reshape(slots * 6, M)
-    old = old_part(velocity, pressure, viscosity)
+    old, edge_low, edge_high = old_part(velocity, pressure, viscosity)
     partial_grid = spread(arrived)
     other_grid = lax.ppermute(partial_grid, "struct", [(0, 1), (1, 0)])
     rim = 3 * YP
@@ -395,17 +446,19 @@
     from_right = shift(low, "fluid", -1)
     folded, low, high = pl.pallas_call(
         fold_kernel,
-        out_shape=(shape((ROWS, lanes), f32), shape((24, lanes), bf16), shape((24, lanes), bf16)),
-        in_specs=[VMEM] * 3,
+        out_shape=(shape((ROWS, lanes), f32), shape((40, lanes), bf16), shape((40, lanes), bf16)),
+        in_specs=[VMEM] * 5,
         out_specs=(VMEM,) * 3,
-        scratch_shapes=[pltpu.VMEM((24, lanes), f32)] * 2,
+        scratch_shapes=[pltpu.VMEM((40, lanes), f32)] * 2,
         compiler_params=grant(6),
         name="fold",
-    )(summed, from_left, from_right)
+    )(summed, from_left, from_right, edge_low, edge_high)
     from_below = shift(high, "sub", 1)
     from_above = shift(low, "sub", -1)
     place = jnp.stack([lax.axis_index("fluid"), lax.axis_index("sub")]).astype(jnp.int32)
-    fresh, sampled = sample(slabs, subs, place, arrived, folded, from_below, from_above)
+    fresh, sampled = sample(
+        slabs, subs, place, arrived, folded, from_below, from_above, edge_low, edge_high
+    )
     returned = lax.all_to_all(
         sampled.reshape(slabs, 3, 2, M), "fluid", split_axis=0, concat_axis=0, tiled=True
     ).reshape(slots * 3, M)

time: 105 us -> 106 us (level)
  starting transfers between devices: 40.6 us -> 34.5 us
  waiting for transfers between devices: 20.4 us -> 25.6 us
  blocking collectives: 22 us -> 25.2 us
  other arithmetic: 1.33 us -> 0.13 us
    ppermute x8 -> x6, starting transfers between devices: 21.9 us -> 15.8 us  [shift(): return lax.ppermute(array, axis, pairs)]
    all_to_all x1, waiting for transfers between devices: 10.5 us -> 15 us  [body(): lax.all_to_all(payload.reshape(slabs, 3, 4, M), 'fluid', split_axis=0, co...]
    all_to_all x1, blocking collectives: 22 us -> 25.2 us  [body(): lax.all_to_all(sampled.reshape(slabs, 3, 2, M), 'fluid', split_axis=0, co...]
    ppermute x8 -> x6, waiting for transfers between devices: 8.73 us -> 10.6 us  [shift(): return lax.ppermute(array, axis, pairs)]
    ppermute x1, waiting for transfers between devices: 1.11 us -> 0.01 us  [body(): other_grid = lax.ppermute(partial_grid, 'struct', [(0, 1), (1, 0)])]
  transfers between devices with their start and end apart: 10 -> 8, of which waited for: 5 -> 6; matrix products, arithmetic and copies ran while one was open for 1% -> 0% of each run, Pallas kernels for 8% -> 8%
where the time goes in v3:
time: 106 us
  starting transfers between devices  34.5 us (33%)
  waiting for transfers between devices  25.6 us (24%)
  blocking collectives  25.2 us (24%)
  Pallas kernels  18.2 us (17%)
  local copies, waits for them, and re-layouts  1.49 us (1%)
    all_to_all x1, blocking collectives, body(): lax.all_to_all(sampled.reshape(slabs, 3, 2, M), 'fluid', split_axis=0, co...  25.2 us
    all_to_all x1, starting transfers between devices, body(): lax.all_to_all(payload.reshape(slabs, 3, 4, M), 'fluid', split_axis=0, co...  16.7 us
    ppermute x6, starting transfers between devices, shift(): return lax.ppermute(array, axis, pairs)  15.8 us
    all_to_all x1, waiting for transfers between devices, body(): lax.all_to_all(payload.reshape(slabs, 3, 4, M), 'fluid', split_axis=0, co...  15 us
    ppermute x6, waiting for transfers between devices, shift(): return lax.ppermute(array, axis, pairs)  10.6 us
    pallas_call x1, Pallas kernels, spread(): pl.pallas_call(spread_kernel, out_shape=jax.ShapeDtypeStruct((ROWS_PAD, 3...  7.96 us
    pallas_call x1, Pallas kernels, sample(): pl.pallas_call(lambda *refs: sample_kernel(slabs, subs, *refs), out_shape...  6.27 us
  transfers between devices with their start and end apart: 8, of which 6 were waited for; matrix products, arithmetic and copies ran while one was open for 0% of the time, Pallas kernels for 8%

profile of v3, /device:TPU:2, one launch (start us, length us, event | category | flops | bytes accessed | tf_op | source)
XLA Modules:
  0.0 105.9 jit_solution(4675848016347043159)
XLA Ops:
  0.6 2.1 %pack.1 = (f32[768,128]{1,0:T(8,128)}, s32[64]{0:T(128)}) custom-call(s32[64]{0:T(128)} %bitcast.32, f32[3,64,128]{2,1,0:T(8,128)} %bitcast.28, s32[3,64,128]{2,1,0:T(8,128)} %bitcast.29, f32[3,64,128]{2,1,0:T(8,128)} %bitcast.30), custom_call_target="tpu_custom_call" | custom-call | tf_op jit(solution)/shard_map/pack/pallas_call | solution.py:418
  2.8 16.7 %all-to-all-start = ((f32[64,3,4,128]{3,2,1,0:T(4,128)}), f32[64,3,4,128]{3,2,1,0:T(4,128)S(1)}, u32[]{:S(2)}, u32[]{:S(2)}) async-start(f32[64,3,4,128]{3,2,1,0:T(4,128)} %bitcast.27), calls=%async_computation | async-start | bytes 786432 | tf_op jit(solution)/shard_map/all_to_all | solution.py:430
  19.6 0.9 copy-done
  20.5 1.3 %collective-permute-start.2 = (bf16[2,5,16,256]{3,2,1,0:T(8,128)(2,1)S(1)}, bf16[2,5,16,256]{3,2,1,0:T(8,128)(2,1)S(1)}, u32[]{:S(2)}, u32[]{:S(2)}) collective-permute-start(bf16[2,5,16,256]{3,2,1,0:T(8,128)(2,1)S(1)} %pad_maximum_fusion), channel_id=1, source_target_pairs={{8,0},{16,8},{24,16},{32,24},{40,32},{48,40},{56,48},{64,56},{72,6... | collective-permute-start | bytes 245768 | tf_op jit(solution)/shard_map/ppermute | solution.py:312
  21.8 15.0 %all-to-all-done = f32[64,3,4,128]{3,2,1,0:T(4,128)S(1)} async-done(((f32[64,3,4,128]{3,2,1,0:T(4,128)}), f32[64,3,4,128]{3,2,1,0:T(4,128)S(1)}, u32[]{:S(2)}, u32[]{:S(2)}) %all-to-all-start) | async-done | bytes 393248 | tf_op jit(solution)/shard_map/all_to_all | solution.py:430
  36.9 8.0 %spread.1.mine_ref = bf16[176,768]{1,0:T(8,128)(2,1)S(1)} custom-call(f32[768,128]{1,0:T(8,128)S(1)} %bitcast.22), custom_call_target="tpu_custom_call" | custom-call | tf_op jit(solution)/shard_map/spread/pallas_call | solution.py:369
  44.8 1.9 %collective-permute-start = (bf16[176,768]{1,0:T(8,128)(2,1)S(1)}, bf16[176,768]{1,0:T(8,128)(2,1)S(1)}, u32[]{:S(2)}, u32[]{:S(2)}) collective-permute-start(bf16[176,768]{1,0:T(8,128)(2,1)S(1)} %spread.1.mine_ref), channel_id=1, source_target_pairs={{0,1},{1,0},{2,3},{3,2},{4,5},{5,4},{6,7},{7,6},{8,9},{9,8},{10,11... | collective-permute-start | bytes 811016 | tf_op jit(solution)/shard_map/ppermute | solution.py:435
  46.8 3.2 %collective-permute-start.1 = (bf16[1,5,16,256]{3,2,1,0:T(8,128)(2,1)S(1)}, bf16[1,5,16,256]{3,2,1,0:T(8,128)(2,1)S(1)}, u32[]{:S(2)}, u32[]{:S(2)}) collective-permute-start(bf16[1,5,16,256]{3,2,1,0:T(8,128)(2,1)S(1)} %pad_maximum_fusion.1), channel_id=1, source_target_pairs={{0,8},{8,16},{16,24},{24,32},{32,40},{40,48},{48,56},{56,64},{64,7... | collective-permute-start | bytes 122888 | tf_op jit(solution)/shard_map/ppermute | solution.py:312
  50.0 1.7 %collective-permute-done.1.before_ref = bf16[1,5,16,256]{3,2,1,0:T(8,128)(2,1)S(1)} collective-permute-done((bf16[1,5,16,256]{3,2,1,0:T(8,128)(2,1)S(1)}, bf16[1,5,16,256]{3,2,1,0:T(8,128)(2,1)S(1)}, u32[]{:S(2)}, u32[]{:S(2)}) %collective-permute-start.1) | collective-permute-done | bytes 40992 | tf_op jit(solution)/shard_map/ppermute | solution.py:312
  51.6 0.3 old.1
  52.0 0.2 join.1
  52.1 4.2 %collective-permute-start.3 = (bf16[72,768]{1,0:T(8,128)(2,1)S(1)}, bf16[72,768]{1,0:T(8,128)(2,1)S(1)}, u32[]{:S(2)}, u32[]{:S(2)}) collective-permute-start(bf16[72,768]{1,0:T(8,128)(2,1)S(1)} %get-tuple-element.26), channel_id=1, source_target_pairs={{0,8},{8,16},{16,24},{24,32},{32,40},{40,48},{48,56},{56,64},{64,7... | collective-permute-start | bytes 331784 | tf_op jit(solution)/shard_map/ppermute | solution.py:312
  56.4 1.3 %collective-permute-start.4 = (bf16[72,768]{1,0:T(8,128)(2,1)S(1)}, bf16[72,768]{1,0:T(8,128)(2,1)S(1)}, u32[]{:S(2)}, u32[]{:S(2)}) collective-permute-start(bf16[72,768]{1,0:T(8,128)(2,1)S(1)} %get-tuple-element.27), channel_id=1, source_target_pairs={{8,0},{16,8},{24,16},{32,24},{40,32},{48,40},{56,48},{64,56},{72,6... | collective-permute-start | bytes 331784 | tf_op jit(solution)/shard_map/ppermute | solution.py:312
  57.7 1.0 collective-permute-done.3.left_ref
  58.7 4.3 %collective-permute-done.4.right_ref = bf16[72,768]{1,0:T(8,128)(2,1)S(1)} collective-permute-done((bf16[72,768]{1,0:T(8,128)(2,1)S(1)}, bf16[72,768]{1,0:T(8,128)(2,1)S(1)}, u32[]{:S(2)}, u32[]{:S(2)}) %collective-permute-start.4) | collective-permute-done | bytes 110624 | tf_op jit(solution)/shard_map/ppermute | solution.py:312
  63.0 0.1 fold.1
  63.1 3.4 %collective-permute-start.5 = (bf16[40,768]{1,0:T(8,128)(2,1)S(1)}, bf16[40,768]{1,0:T(8,128)(2,1)S(1)}, u32[]{:S(2)}, u32[]{:S(2)}) collective-permute-start(bf16[40,768]{1,0:T(8,128)(2,1)S(1)} %get-tuple-element.31), channel_id=1, source_target_pairs={{0,2},{2,4},{4,6},{1,3},{3,5},{5,7},{8,10},{10,12},{12,14},{9,11},... | collective-permute-start | bytes 184328 | tf_op jit(solution)/shard_map/ppermute | solution.py:312
  66.5 2.5 %collective-permute-start.6 = (bf16[40,768]{1,0:T(8,128)(2,1)S(1)}, bf16[40,768]{1,0:T(8,128)(2,1)S(1)}, u32[]{:S(2)}, u32[]{:S(2)}) collective-permute-start(bf16[40,768]{1,0:T(8,128)(2,1)S(1)} %get-tuple-element.32), channel_id=1, source_target_pairs={{2,0},{4,2},{6,4},{3,1},{5,3},{7,5},{10,8},{12,10},{14,12},{11,9},... | collective-permute-start | bytes 184328 | tf_op jit(solution)/shard_map/ppermute | solution.py:312
  69.1 0.2 collective-permute-done.5.refs_3_
  69.2 3.4 %collective-permute-done.6.refs_4_ = bf16[40,768]{1,0:T(8,128)(2,1)S(1)} collective-permute-done((bf16[40,768]{1,0:T(8,128)(2,1)S(1)}, bf16[40,768]{1,0:T(8,128)(2,1)S(1)}, u32[]{:S(2)}, u32[]{:S(2)}) %collective-permute-start.6) | collective-permute-done | bytes 61472 | tf_op jit(solution)/shard_map/ppermute | solution.py:312
  72.6 6.3 %sample.1 = (f32[4,3,16,256]{3,2,1,0:T(8,128)}, f32[384,128]{1,0:T(8,128)S(1)}) custom-call(s32[2]{0:T(128)S(1)} %pad_add_fusion.refs_0_, f32[768,128]{1,0:T(8,128)S(1)} %bitcast.23, f32[168,768]{1,0:T(8,128)S(1)} %get-tuple-element.30.refs_2_, bf16[40,768]{1,0:T(8,128)(2,1)S(1)} %collective-permute-done.5.refs_3_, ...), custom_call_target="tpu_custom_call" | custom-call | tf_op jit(solution)/shard_map/sample/pallas_call | solution.py:387
  78.9 25.2 %all_to_all.10 = f32[64,3,2,128]{3,2,1,0:T(2,128)S(1)} all-to-all(f32[64,3,2,128]{3,2,1,0:T(2,128)S(1)} %bitcast.26), channel_id=1, replica_groups=mesh['fluid'=64,'sub'=4,'struct'=2] {'fluid'}, dimensions={0} | all-to-all | bytes 393216 | tf_op jit(solution)/shard_map/all_to_all | solution.py:462
  104.1 0.6 copy-done.3
  104.6 1.3 %take.1 = f32[3,64,128]{2,1,0:T(8,128)} custom-call(s32[64]{0:T(128)S(1)} %copy-done.3, f32[384,128]{1,0:T(8,128)S(1)} %bitcast.25), custom_call_target="tpu_custom_call" | custom-call | tf_op jit(solution)/shard_map/take/pallas_call | solution.py:465
  (21 shorter events, 0.2 us)
Async XLA Ops:
  2.7 16.8 %copy-start.1 = (f32[4,16,256]{2,1,0:T(8,128)S(1)}, f32[4,16,256]{2,1,0:T(8,128)}, u32[]{:S(2)}) copy-start(f32[4,16,256]{2,1,0:T(8,128)} %p_ref) | copy-start | bytes 196612
  2.7 16.8 %copy-start.2 = (f32[4,16,256]{2,1,0:T(8,128)S(1)}, f32[4,16,256]{2,1,0:T(8,128)}, u32[]{:S(2)}) copy-start(f32[4,16,256]{2,1,0:T(8,128)} %n_ref) | copy-start | bytes 196612
  2.8 34.1 %all-to-all-start = ((f32[64,3,4,128]{3,2,1,0:T(4,128)}), f32[64,3,4,128]{3,2,1,0:T(4,128)S(1)}, u32[]{:S(2)}, u32[]{:S(2)}) async-start(f32[64,3,4,128]{3,2,1,0:T(4,128)} %bitcast.27), calls=%async_computation | async-start | bytes 786432 | tf_op jit(solution)/shard_map/all_to_all | solution.py:430
  19.5 0.9 copy-start
  20.5 1.4 %copy-start.4 = (bf16[4,3,16,256]{3,2,1,0:T(8,128)(2,1)}, bf16[4,3,16,256]{3,2,1,0:T(8,128)(2,1)S(1)}, u32[]{:S(2)}) copy-start(bf16[4,3,16,256]{3,2,1,0:T(8,128)(2,1)S(1)} %bitcast_convert_fusion) | copy-start | bytes 294916
  20.5 31.1 %collective-permute-start.2 = (bf16[2,5,16,256]{3,2,1,0:T(8,128)(2,1)S(1)}, bf16[2,5,16,256]{3,2,1,0:T(8,128)(2,1)S(1)}, u32[]{:S(2)}, u32[]{:S(2)}) collective-permute-start(bf16[2,5,16,256]{3,2,1,0:T(8,128)(2,1)S(1)} %pad_maximum_fusion), channel_id=1, source_target_pairs={{8,0},{16,8},{24,16},{32,24},{40,32},{48,40},{56,48},{64,56},{72,6... | collective-permute-start | bytes 245768 | tf_op jit(solution)/shard_map/ppermute | solution.py:312
  44.8 2.0 %slice-start = ((bf16[4,3,16,256]{3,2,1,0:T(8,128)(2,1)}), bf16[1,3,16,256]{3,2,1,0:T(8,128)(2,1)S(1)}, s32[]{:S(2)}) async-start(bf16[4,3,16,256]{3,2,1,0:T(8,128)(2,1)} %copy-done.4), calls=%async_computation.2 | async-start | bytes 49152 | tf_op jit(solution)/shard_map/slice | solution.py:349
  44.8 7.1 %collective-permute-start = (bf16[176,768]{1,0:T(8,128)(2,1)S(1)}, bf16[176,768]{1,0:T(8,128)(2,1)S(1)}, u32[]{:S(2)}, u32[]{:S(2)}) collective-permute-start(bf16[176,768]{1,0:T(8,128)(2,1)S(1)} %spread.1.mine_ref), channel_id=1, source_target_pairs={{0,1},{1,0},{2,3},{3,2},{4,5},{5,4},{6,7},{7,6},{8,9},{9,8},{10,11... | collective-permute-start | bytes 811016 | tf_op jit(solution)/shard_map/ppermute | solution.py:435
  46.8 4.8 %collective-permute-start.1 = (bf16[1,5,16,256]{3,2,1,0:T(8,128)(2,1)S(1)}, bf16[1,5,16,256]{3,2,1,0:T(8,128)(2,1)S(1)}, u32[]{:S(2)}, u32[]{:S(2)}) collective-permute-start(bf16[1,5,16,256]{3,2,1,0:T(8,128)(2,1)S(1)} %pad_maximum_fusion.1), channel_id=1, source_target_pairs={{0,8},{8,16},{16,24},{24,32},{32,40},{40,48},{48,56},{56,64},{64,7... | collective-permute-start | bytes 122888 | tf_op jit(solution)/shard_map/ppermute | solution.py:312
  52.1 6.6 %collective-permute-start.3 = (bf16[72,768]{1,0:T(8,128)(2,1)S(1)}, bf16[72,768]{1,0:T(8,128)(2,1)S(1)}, u32[]{:S(2)}, u32[]{:S(2)}) collective-permute-start(bf16[72,768]{1,0:T(8,128)(2,1)S(1)} %get-tuple-element.26), channel_id=1, source_target_pairs={{0,8},{8,16},{16,24},{24,32},{32,40},{40,48},{48,56},{56,64},{64,7... | collective-permute-start | bytes 331784 | tf_op jit(solution)/shard_map/ppermute | solution.py:312
  56.4 6.6 %collective-permute-start.4 = (bf16[72,768]{1,0:T(8,128)(2,1)S(1)}, bf16[72,768]{1,0:T(8,128)(2,1)S(1)}, u32[]{:S(2)}, u32[]{:S(2)}) collective-permute-start(bf16[72,768]{1,0:T(8,128)(2,1)S(1)} %get-tuple-element.27), channel_id=1, source_target_pairs={{8,0},{16,8},{24,16},{32,24},{40,32},{48,40},{56,48},{64,56},{72,6... | collective-permute-start | bytes 331784 | tf_op jit(solution)/shard_map/ppermute | solution.py:312
  63.1 6.1 %collective-permute-start.5 = (bf16[40,768]{1,0:T(8,128)(2,1)S(1)}, bf16[40,768]{1,0:T(8,128)(2,1)S(1)}, u32[]{:S(2)}, u32[]{:S(2)}) collective-permute-start(bf16[40,768]{1,0:T(8,128)(2,1)S(1)} %get-tuple-element.31), channel_id=1, source_target_pairs={{0,2},{2,4},{4,6},{1,3},{3,5},{5,7},{8,10},{10,12},{12,14},{9,11},... | collective-permute-start | bytes 184328 | tf_op jit(solution)/shard_map/ppermute | solution.py:312
  66.5 6.1 %collective-permute-start.6 = (bf16[40,768]{1,0:T(8,128)(2,1)S(1)}, bf16[40,768]{1,0:T(8,128)(2,1)S(1)}, u32[]{:S(2)}, u32[]{:S(2)}) collective-permute-start(bf16[40,768]{1,0:T(8,128)(2,1)S(1)} %get-tuple-element.32), channel_id=1, source_target_pairs={{2,0},{4,2},{6,4},{3,1},{5,3},{7,5},{10,8},{12,10},{14,12},{11,9},... | collective-permute-start | bytes 184328 | tf_op jit(solution)/shard_map/ppermute | solution.py:312
  104.1 0.6 copy-start.3

commit v4 on v3

--- a/solution.py
+++ b/solution.py
@@ -343,13 +343,28 @@
             out_ref[x - 1, c] = total
 
 
+def edge_kernel(v_ref, p_ref, n_ref, first_ref, last_ref):
+    for ref, start in ((first_ref, 0), (last_ref, v_ref.shape[0] - 1)):
+        for x in range(ref.shape[0]):
+            for c in range(3):
+                ref[x, c] = v_ref[start + x, c].astype(jnp.bfloat16)
+            ref[x, 3] = p_ref[start + x].astype(jnp.bfloat16)
+            ref[x, 4] = n_ref[start + x].astype(jnp.bfloat16)
+
+
 def old_part(velocity, pressure, viscosity):
     v = jnp.transpose(velocity, (0, 2, 1, 3))
-    picked = lambda rows: jnp.concatenate(
-        [v[rows], pressure[rows][:, None], viscosity[rows][:, None]], axis=1
-    ).astype(jnp.bfloat16)
-    before = shift(picked(slice(3, 4)), "fluid", 1)
-    after = shift(picked(slice(0, 2)), "fluid", -1)
+    rows = lambda count: jax.ShapeDtypeStruct((count, 5, *v.shape[2:]), jnp.bfloat16)
+    first, last = pl.pallas_call(
+        edge_kernel,
+        out_shape=(rows(2), rows(1)),
+        in_specs=[VMEM] * 3,
+        out_specs=(VMEM, VMEM),
+        compiler_params=grant(50),
+        name="edge",
+    )(v, pressure, viscosity)
+    before = shift(last, "fluid", 1)
+    after = shift(first, "fluid", -1)
     edge = jax.ShapeDtypeStruct((XE + 1, 5 * NZ), jnp.float32)
     return pl.pallas_call(
         old_kernel,
@@ -424,9 +439,6 @@
         compiler_params=grant(60),
         name="pack",
     )(block_slab[:, 0], swap01(marker_offset), swap01(cell_base), swap01(marker_force))
-    payload, velocity, pressure, viscosity = lax.optimization_barrier(
-        (payload, velocity, pressure, viscosity)
-    )
     arrived = lax.all_to_all(
         payload.reshape(slabs, 3, 4, M), "fluid", split_axis=0, concat_axis=0, tiled=True
     ).reshape(slots * 6, M)

time: 106 us -> 110 us (1.038)
  blocking collectives: 25.2 us -> 60.6 us
  starting transfers between devices: 34.5 us -> 19.1 us
  waiting for transfers between devices: 25.6 us -> 10.6 us
    all_to_all x0 -> x1, blocking collectives: none -> 34 us  [body(): lax.all_to_all(payload.reshape(slabs, 3, 4, M), 'fluid', split_axis=0, co...]
    all_to_all x1 -> x0, starting transfers between devices: 16.7 us -> none  [body(): lax.all_to_all(payload.reshape(slabs, 3, 4, M), 'fluid', split_axis=0, co...]
    all_to_all x1 -> x0, waiting for transfers between devices: 15 us -> none  [body(): lax.all_to_all(payload.reshape(slabs, 3, 4, M), 'fluid', split_axis=0, co...]
    all_to_all x1, blocking collectives: 25.2 us -> 26.6 us  [body(): lax.all_to_all(sampled.reshape(slabs, 3, 2, M), 'fluid', split_axis=0, co...]
    ppermute x6, starting transfers between devices: 15.8 us -> 17.2 us  [shift(): return lax.ppermute(array, axis, pairs)]
  transfers between devices with their start and end apart: 8 -> 7, of which waited for: 6 -> 5; matrix products, arithmetic and copies ran while one was open for 0% -> 0% of each run, Pallas kernels for 8% -> 0%
where the time goes in v4:
time: 110 us
  blocking collectives  60.6 us (55%)
  starting transfers between devices  19.1 us (17%)
  Pallas kernels  18.2 us (17%)
  waiting for transfers between devices  10.6 us (10%)
    all_to_all x1, blocking collectives, body(): lax.all_to_all(payload.reshape(slabs, 3, 4, M), 'fluid', split_axis=0, co...  34 us
    all_to_all x1, blocking collectives, body(): lax.all_to_all(sampled.reshape(slabs, 3, 2, M), 'fluid', split_axis=0, co...  26.6 us
    ppermute x6, starting transfers between devices, shift(): return lax.ppermute(array, axis, pairs)  17.2 us
    ppermute x6, waiting for transfers between devices, shift(): return lax.ppermute(array, axis, pairs)  10.6 us
    pallas_call x1, Pallas kernels, spread(): pl.pallas_call(spread_kernel, out_shape=jax.ShapeDtypeStruct((ROWS_PAD, 3...  7.95 us
    pallas_call x1, Pallas kernels, sample(): pl.pallas_call(lambda *refs: sample_kernel(slabs, subs, *refs), out_shape...  6.26 us
  transfers between devices with their start and end apart: 7, of which 5 were waited for; matrix products, arithmetic and copies ran while one was open for 0% of the time, Pallas kernels for 0%

profile of v4, /device:TPU:2, one launch (start us, length us, event | category | flops | bytes accessed | tf_op | source)
XLA Modules:
  0.0 110.0 jit_solution(4151323657729955575)
XLA Ops:
  0.6 2.1 %pack.1 = (f32[768,128]{1,0:T(8,128)}, s32[64]{0:T(128)}) custom-call(s32[64]{0:T(128)} %bitcast.24, f32[3,64,128]{2,1,0:T(8,128)} %bitcast.20, s32[3,64,128]{2,1,0:T(8,128)} %bitcast.21, f32[3,64,128]{2,1,0:T(8,128)} %bitcast.22), custom_call_target="tpu_custom_call" | custom-call | tf_op jit(solution)/shard_map/pack/pallas_call | solution.py:433
  2.7 34.0 %all_to_all.10 = f32[64,3,4,128]{3,2,1,0:T(4,128)S(1)} all-to-all(f32[64,3,4,128]{3,2,1,0:T(4,128)} %bitcast.19), channel_id=1, replica_groups=mesh['fluid'=64,'sub'=4,'struct'=2] {'fluid'}, dimensions={0} | all-to-all | bytes 786432 | tf_op jit(solution)/shard_map/all_to_all | solution.py:442
  36.7 8.0 %spread.1.mine_ref = bf16[176,768]{1,0:T(8,128)(2,1)S(1)} custom-call(f32[768,128]{1,0:T(8,128)S(1)} %bitcast.13), custom_call_target="tpu_custom_call" | custom-call | tf_op jit(solution)/shard_map/spread/pallas_call | solution.py:384
  44.7 1.9 %collective-permute-start = (bf16[176,768]{1,0:T(8,128)(2,1)S(1)}, bf16[176,768]{1,0:T(8,128)(2,1)S(1)}, u32[]{:S(2)}, u32[]{:S(2)}) collective-permute-start(bf16[176,768]{1,0:T(8,128)(2,1)S(1)} %spread.1.mine_ref), channel_id=1, source_target_pairs={{0,1},{1,0},{2,3},{3,2},{4,5},{5,4},{6,7},{7,6},{8,9},{9,8},{10,11... | collective-permute-start | bytes 811016 | tf_op jit(solution)/shard_map/ppermute | solution.py:447
  46.6 1.3 %collective-permute-start.2 = (bf16[2,5,16,256]{3,2,1,0:T(8,128)(2,1)S(1)}, bf16[2,5,16,256]{3,2,1,0:T(8,128)(2,1)S(1)}, u32[]{:S(2)}, u32[]{:S(2)}) collective-permute-start(bf16[2,5,16,256]{3,2,1,0:T(8,128)(2,1)S(1)} %get-tuple-element.19), channel_id=1, source_target_pairs={{8,0},{16,8},{24,16},{32,24},{40,32},{48,40},{56,48},{64,56},{72,6... | collective-permute-start | bytes 245768 | tf_op jit(solution)/shard_map/ppermute | solution.py:312
  47.9 4.5 %collective-permute-start.1 = (bf16[1,5,16,256]{3,2,1,0:T(8,128)(2,1)S(1)}, bf16[1,5,16,256]{3,2,1,0:T(8,128)(2,1)S(1)}, u32[]{:S(2)}, u32[]{:S(2)}) collective-permute-start(bf16[1,5,16,256]{3,2,1,0:T(8,128)(2,1)S(1)} %get-tuple-element.18), channel_id=1, source_target_pairs={{0,8},{8,16},{16,24},{24,32},{32,40},{40,48},{48,56},{56,64},{64,7... | collective-permute-start | bytes 122888 | tf_op jit(solution)/shard_map/ppermute | solution.py:312
  52.5 1.7 %collective-permute-done.1.before_ref = bf16[1,5,16,256]{3,2,1,0:T(8,128)(2,1)S(1)} collective-permute-done((bf16[1,5,16,256]{3,2,1,0:T(8,128)(2,1)S(1)}, bf16[1,5,16,256]{3,2,1,0:T(8,128)(2,1)S(1)}, u32[]{:S(2)}, u32[]{:S(2)}) %collective-permute-start.1) | collective-permute-done | bytes 40992 | tf_op jit(solution)/shard_map/ppermute | solution.py:312
  54.2 0.0 collective-permute-done.2.after_ref
  54.2 0.3 old.1
  54.5 0.2 join.1
  54.7 4.2 %collective-permute-start.3 = (bf16[72,768]{1,0:T(8,128)(2,1)S(1)}, bf16[72,768]{1,0:T(8,128)(2,1)S(1)}, u32[]{:S(2)}, u32[]{:S(2)}) collective-permute-start(bf16[72,768]{1,0:T(8,128)(2,1)S(1)} %get-tuple-element.22), channel_id=1, source_target_pairs={{0,8},{8,16},{16,24},{24,32},{32,40},{40,48},{48,56},{56,64},{64,7... | collective-permute-start | bytes 331784 | tf_op jit(solution)/shard_map/ppermute | solution.py:312
  58.9 1.3 %collective-permute-start.4 = (bf16[72,768]{1,0:T(8,128)(2,1)S(1)}, bf16[72,768]{1,0:T(8,128)(2,1)S(1)}, u32[]{:S(2)}, u32[]{:S(2)}) collective-permute-start(bf16[72,768]{1,0:T(8,128)(2,1)S(1)} %get-tuple-element.23), channel_id=1, source_target_pairs={{8,0},{16,8},{24,16},{32,24},{40,32},{48,40},{56,48},{64,56},{72,6... | collective-permute-start | bytes 331784 | tf_op jit(solution)/shard_map/ppermute | solution.py:312
  60.2 1.0 collective-permute-done.3.left_ref
  61.2 4.3 %collective-permute-done.4.right_ref = bf16[72,768]{1,0:T(8,128)(2,1)S(1)} collective-permute-done((bf16[72,768]{1,0:T(8,128)(2,1)S(1)}, bf16[72,768]{1,0:T(8,128)(2,1)S(1)}, u32[]{:S(2)}, u32[]{:S(2)}) %collective-permute-start.4) | collective-permute-done | bytes 110624 | tf_op jit(solution)/shard_map/ppermute | solution.py:312
  65.5 0.1 fold.1
  65.7 3.4 %collective-permute-start.5 = (bf16[40,768]{1,0:T(8,128)(2,1)S(1)}, bf16[40,768]{1,0:T(8,128)(2,1)S(1)}, u32[]{:S(2)}, u32[]{:S(2)}) collective-permute-start(bf16[40,768]{1,0:T(8,128)(2,1)S(1)} %get-tuple-element.27), channel_id=1, source_target_pairs={{0,2},{2,4},{4,6},{1,3},{3,5},{5,7},{8,10},{10,12},{12,14},{9,11},... | collective-permute-start | bytes 184328 | tf_op jit(solution)/shard_map/ppermute | solution.py:312
  69.1 2.4 %collective-permute-start.6 = (bf16[40,768]{1,0:T(8,128)(2,1)S(1)}, bf16[40,768]{1,0:T(8,128)(2,1)S(1)}, u32[]{:S(2)}, u32[]{:S(2)}) collective-permute-start(bf16[40,768]{1,0:T(8,128)(2,1)S(1)} %get-tuple-element.28), channel_id=1, source_target_pairs={{2,0},{4,2},{6,4},{3,1},{5,3},{7,5},{10,8},{12,10},{14,12},{11,9},... | collective-permute-start | bytes 184328 | tf_op jit(solution)/shard_map/ppermute | solution.py:312
  71.5 0.1 pad_add_fusion.refs_0_
  71.6 0.2 collective-permute-done.5.refs_3_
  71.8 3.4 %collective-permute-done.6.refs_4_ = bf16[40,768]{1,0:T(8,128)(2,1)S(1)} collective-permute-done((bf16[40,768]{1,0:T(8,128)(2,1)S(1)}, bf16[40,768]{1,0:T(8,128)(2,1)S(1)}, u32[]{:S(2)}, u32[]{:S(2)}) %collective-permute-start.6) | collective-permute-done | bytes 61472 | tf_op jit(solution)/shard_map/ppermute | solution.py:312
  75.2 6.3 %sample.1 = (f32[4,3,16,256]{3,2,1,0:T(8,128)}, f32[384,128]{1,0:T(8,128)S(1)}) custom-call(s32[2]{0:T(128)S(1)} %pad_add_fusion.refs_0_, f32[768,128]{1,0:T(8,128)S(1)} %bitcast.14, f32[168,768]{1,0:T(8,128)S(1)} %get-tuple-element.26.refs_2_, bf16[40,768]{1,0:T(8,128)(2,1)S(1)} %collective-permute-done.5.refs_3_, ...), custom_call_target="tpu_custom_call" | custom-call | tf_op jit(solution)/shard_map/sample/pallas_call | solution.py:402
  81.5 26.6 %all_to_all.11 = f32[64,3,2,128]{3,2,1,0:T(2,128)S(1)} all-to-all(f32[64,3,2,128]{3,2,1,0:T(2,128)S(1)} %bitcast.18), channel_id=1, replica_groups=mesh['fluid'=64,'sub'=4,'struct'=2] {'fluid'}, dimensions={0} | all-to-all | bytes 393216 | tf_op jit(solution)/shard_map/all_to_all | solution.py:474
  108.1 0.7 copy-done.3
  108.7 1.3 %take.1 = f32[3,64,128]{2,1,0:T(8,128)} custom-call(s32[64]{0:T(128)S(1)} %copy-done.3, f32[384,128]{1,0:T(8,128)S(1)} %bitcast.17), custom_call_target="tpu_custom_call" | custom-call | tf_op jit(solution)/shard_map/take/pallas_call | solution.py:477
  (9 shorter events, 0.0 us)
Async XLA Ops:
  36.7 9.9 %copy-start = (f32[4,16,3,256]{3,1,2,0:T(8,128)S(1)}, f32[4,16,3,256]{3,1,2,0:T(8,128)}, u32[]{:S(2)}) copy-start(f32[4,16,3,256]{3,1,2,0:T(8,128)} %param.7) | copy-start | bytes 589828
  36.7 9.9 %copy-start.1 = (f32[4,16,256]{2,1,0:T(8,128)S(1)}, f32[4,16,256]{2,1,0:T(8,128)}, u32[]{:S(2)}) copy-start(f32[4,16,256]{2,1,0:T(8,128)} %p_ref.3) | copy-start | bytes 196612
  36.7 9.9 %copy-start.2 = (f32[4,16,256]{2,1,0:T(8,128)S(1)}, f32[4,16,256]{2,1,0:T(8,128)}, u32[]{:S(2)}) copy-start(f32[4,16,256]{2,1,0:T(8,128)} %n_ref.3) | copy-start | bytes 196612
  44.7 9.8 %collective-permute-start = (bf16[176,768]{1,0:T(8,128)(2,1)S(1)}, bf16[176,768]{1,0:T(8,128)(2,1)S(1)}, u32[]{:S(2)}, u32[]{:S(2)}) collective-permute-start(bf16[176,768]{1,0:T(8,128)(2,1)S(1)} %spread.1.mine_ref), channel_id=1, source_target_pairs={{0,1},{1,0},{2,3},{3,2},{4,5},{5,4},{6,7},{7,6},{8,9},{9,8},{10,11... | collective-permute-start | bytes 811016 | tf_op jit(solution)/shard_map/ppermute | solution.py:447
  46.6 7.5 %collective-permute-start.2 = (bf16[2,5,16,256]{3,2,1,0:T(8,128)(2,1)S(1)}, bf16[2,5,16,256]{3,2,1,0:T(8,128)(2,1)S(1)}, u32[]{:S(2)}, u32[]{:S(2)}) collective-permute-start(bf16[2,5,16,256]{3,2,1,0:T(8,128)(2,1)S(1)} %get-tuple-element.19), channel_id=1, source_target_pairs={{8,0},{16,8},{24,16},{32,24},{40,32},{48,40},{56,48},{64,56},{72,6... | collective-permute-start | bytes 245768 | tf_op jit(solution)/shard_map/ppermute | solution.py:312
  47.9 6.2 %collective-permute-start.1 = (bf16[1,5,16,256]{3,2,1,0:T(8,128)(2,1)S(1)}, bf16[1,5,16,256]{3,2,1,0:T(8,128)(2,1)S(1)}, u32[]{:S(2)}, u32[]{:S(2)}) collective-permute-start(bf16[1,5,16,256]{3,2,1,0:T(8,128)(2,1)S(1)} %get-tuple-element.18), channel_id=1, source_target_pairs={{0,8},{8,16},{16,24},{24,32},{32,40},{40,48},{48,56},{56,64},{64,7... | collective-permute-start | bytes 122888 | tf_op jit(solution)/shard_map/ppermute | solution.py:312
  54.7 6.6 %collective-permute-start.3 = (bf16[72,768]{1,0:T(8,128)(2,1)S(1)}, bf16[72,768]{1,0:T(8,128)(2,1)S(1)}, u32[]{:S(2)}, u32[]{:S(2)}) collective-permute-start(bf16[72,768]{1,0:T(8,128)(2,1)S(1)} %get-tuple-element.22), channel_id=1, source_target_pairs={{0,8},{8,16},{16,24},{24,32},{32,40},{40,48},{48,56},{56,64},{64,7... | collective-permute-start | bytes 331784 | tf_op jit(solution)/shard_map/ppermute | solution.py:312
  58.9 6.6 %collective-permute-start.4 = (bf16[72,768]{1,0:T(8,128)(2,1)S(1)}, bf16[72,768]{1,0:T(8,128)(2,1)S(1)}, u32[]{:S(2)}, u32[]{:S(2)}) collective-permute-start(bf16[72,768]{1,0:T(8,128)(2,1)S(1)} %get-tuple-element.23), channel_id=1, source_target_pairs={{8,0},{16,8},{24,16},{32,24},{40,32},{48,40},{56,48},{64,56},{72,6... | collective-permute-start | bytes 331784 | tf_op jit(solution)/shard_map/ppermute | solution.py:312
  65.7 6.1 %collective-permute-start.5 = (bf16[40,768]{1,0:T(8,128)(2,1)S(1)}, bf16[40,768]{1,0:T(8,128)(2,1)S(1)}, u32[]{:S(2)}, u32[]{:S(2)}) collective-permute-start(bf16[40,768]{1,0:T(8,128)(2,1)S(1)} %get-tuple-element.27), channel_id=1, source_target_pairs={{0,2},{2,4},{4,6},{1,3},{3,5},{5,7},{8,10},{10,12},{12,14},{9,11},... | collective-permute-start | bytes 184328 | tf_op jit(solution)/shard_map/ppermute | solution.py:312
  69.1 6.1 %collective-permute-start.6 = (bf16[40,768]{1,0:T(8,128)(2,1)S(1)}, bf16[40,768]{1,0:T(8,128)(2,1)S(1)}, u32[]{:S(2)}, u32[]{:S(2)}) collective-permute-start(bf16[40,768]{1,0:T(8,128)(2,1)S(1)} %get-tuple-element.28), channel_id=1, source_target_pairs={{2,0},{4,2},{6,4},{3,1},{5,3},{7,5},{10,8},{12,10},{14,12},{11,9},... | collective-permute-start | bytes 184328 | tf_op jit(solution)/shard_map/ppermute | solution.py:312
  108.1 0.7 copy-start.3
